TPU v7x, 128 devices: a whole 4x4x4 slice. The times are simulated.
128 devices in a mesh: gx: 8 (over x, y_hi), gy: 16 (over y_lo, z, core).
Axes of the slice: x: 4, y: 4 (y_hi: 2, y_lo: 2; y = y_hi * 2 + y_lo), z: 4, core: 2. Of those that a mesh axis runs over, the one named last changes fastest.
Arguments:
- probes: bfloat16 [16, 64, 64, 384], P('gx', 'gy'), may hold values from -6 to 6
- counts: int32 [16, 64], P('gx', 'gy'), may hold values from 1 to 128, 3276 in all within a row
- blocks: bfloat16 [16, 64, 9, 384, 384], P('gx', 'gy'), as said below
Outputs:
- displacements: bfloat16 [16, 64, 64, 384], P('gx', 'gy')
- msd: float32 [16, 64, 384], P('gx', 'gy')
Inputs may be any that keep to these rules, and one draw needn't show every extreme that they name: Each row counts[x, :] sums to 3276, and its largest entry is 128. blocks[a, 3 (dx + 1) + (dy + 1)] is the transpose of blocks[a + (dx, dy), 3 (1 - dx) + (1 - dy)] (cells taken periodically), so blocks[a, 4] is symmetric.
All inputs are finite; a program needn't handle non-finite values. No bound on the sum of `counts` on one device may be relied on, other than what follows from the above.
Results may differ from a plain program's by a relative error of at most 0.006.
Values may be sent and summed in bfloat16 or wider, within the bound.
No kernel may reach another device: no remote copies, remote signals or barrier semaphores. Data moves between devices by JAX's collectives and lax.ppermute only.
A program may use at most 64 MiB of HBM per device.

v0:
```python
import math

import jax
import jax.numpy as jnp
import numpy as np
from jax import lax
from jax.experimental import pallas as pl
from jax.experimental.pallas import tpu as pltpu
from jax.sharding import PartitionSpec as P


TERMS = 8


inverse_temp = 4.0
low_band = 0.02
high_band = 1.0

ROWS = 2
COLS = 4
FORWARD = (((1,), (1,)), ((), ()))


def chebyshev_weights(term_count):
    node_count = 64
    values = []
    angles = []
    for n in range(node_count):
        angle = math.pi * (n + 0.5) / node_count
        energy = low_band + (math.cos(angle) + 1.0) * (high_band - low_band) / 2.0
        root_energy = math.sqrt(energy)
        decay = math.exp(-inverse_temp * root_energy)
        values.append((1.0 + decay) / (1.0 - decay) / (2.0 * root_energy))
        angles.append(angle)
    coeffs = []
    for k in range(term_count):
        total = 0.0
        for n in range(node_count):
            total = total + values[n] * math.cos(k * angles[n])
        coeffs.append(2.0 / node_count * total)
    coeffs[0] = coeffs[0] / 2.0
    return [float(np.float32(c)) for c in coeffs]


def place(parity, row, col):
    odd_x = parity[0]
    odd_y = parity[1]
    x = odd_x if row == 0 else 1 - odd_x
    y = (3 - col) + odd_y * (2 * col - 3)
    return x, y


def toward(parity, step_row, step_col):
    odd_x = parity[0]
    odd_y = parity[1]
    dx = (2 * odd_x, 1, 2 - 2 * odd_x)[step_row]
    dy = (2 - 2 * odd_y, 1, 2 * odd_y)[step_col]
    return 3 * dx + dy


def start_kernel(parity, counts, probes, far, near):
    lane = lax.broadcasted_iota(jnp.int32, probes.shape[2:], 1)
    for row, out in enumerate((far, near)):
        for col in range(COLS):
            x, y = place(parity, row, col)
            live = lane < 3 * counts[x, y]
            out[col] = jnp.where(live, probes[x, y].astype(jnp.float32), 0.0).astype(jnp.bfloat16)


def load_kernel(parity, blocks, far, near, out, total, sems):
    cells = [(row, col) for row in range(ROWS) for col in range(COLS)]
    for row, col in cells:
        x, y = place(parity, row, col)
        for step_row in range(3):
            for step_col in range(3):
                pltpu.make_async_copy(
                    blocks.at[x, y, toward(parity, step_row, step_col)],
                    out.at[row, col, 3 * step_row + step_col],
                    sems.at[COLS * row + col],
                ).start()
    for row, col in cells:
        pltpu.make_async_copy(blocks.at[row, col], out.at[row, col], sems.at[COLS * row + col]).wait()
        total[row, col] = own_product(far, near, out, row, col)


def product(blocks, row, col, pieces):
    left = jnp.concatenate([blocks[row, col, slot] for slot, _ in pieces], axis=1)
    right = jnp.concatenate([v for _, v in pieces], axis=1)
    return lax.dot_general(left, right, FORWARD, preferred_element_type=jnp.float32)


def own_product(far, near, blocks, row, col):
    pieces = []
    for other, ref in enumerate((far, near)):
        step_row = other - row + 1
        for step_col in range(3):
            c = col + step_col - 1
            if 0 <= c < COLS:
                pieces.append((3 * step_row + step_col, ref[c]))
    return product(blocks, row, col, pieces)


def own_kernel(far, near, blocks, total):
    for row in range(ROWS):
        for col in range(COLS):
            total[row, col] = own_product(far, near, blocks, row, col)


def row_product(ref, blocks, row, col):
    pieces = []
    for step_col in range(3):
        c = col + step_col - 1
        if 0 <= c < COLS:
            pieces.append((3 * (2 * row) + step_col, ref[c]))
    return product(blocks, row, col, pieces)


def column_product(ref, blocks, row, col):
    step_col = 0 if col == 0 else 2
    return product(blocks, row, col, [(3 * s + step_col, ref[row + s]) for s in range(3)])


def edge_kernel(halo_far, far, near, halo_near, core_edge, chip_edge):
    for slot, ref in enumerate((halo_far, far, near, halo_near)):
        core_edge[slot] = ref[0]
        chip_edge[slot] = ref[COLS - 1]


def advance(index, coeffs, parity, counts, state, cols, slot, row, raw):
    col = cols[slot]
    x, y = place(parity, row, col)
    lane = lax.broadcasted_iota(jnp.int32, raw.shape[::-1], 1)
    applied = jnp.where(lane < 3 * counts[x, y], raw.T, 0.0)
    first = None
    if index in (1, 2, TERMS - 1):
        first = state[-2:][row][col].astype(jnp.float32)
    if index == 1:
        return applied, coeffs[0] * first + coeffs[1] * applied, None
    if index == 2:
        summed, before = state[0][row, slot], first
    else:
        summed, before = state[0][row, slot], state[1][row, slot]
    term = 2.0 * applied - before
    summed = summed + coeffs[index] * term
    msd = None
    if index == TERMS - 1:
        msd = jnp.sum(first * summed, axis=0, keepdims=True) * (1.0 / raw.shape[1])
    return term, summed, msd


def state_size(index):
    return {1: 2, 2: 3, TERMS - 1: 4}.get(index, 2)


def make_rows(index, coeffs):
    def rows(parity, counts, halo_far, halo_near, blocks, partial, *refs):
        state, outs = refs[: state_size(index)], refs[state_size(index) :]
        for row, ref in enumerate((halo_far, halo_near)):
            for col in (1, 2, 0, 3):
                raw = partial[row, col] + row_product(ref, blocks, row, col)
                if col in (0, 3):
                    outs[0 if col == 0 else 1][row] = raw
                    continue
                slot = col - 1
                term, summed, msd = advance(index, coeffs, parity, counts, state, (1, 2), slot, row, raw)
                if index == TERMS - 1:
                    outs[2][row, slot] = summed.astype(jnp.bfloat16)
                    outs[3][row, slot] = msd
                else:
                    outs[2][row, slot] = term.astype(jnp.bfloat16)
                    outs[3][row, slot] = summed
                    outs[4][row, slot] = term

    return rows


def make_core(index, coeffs):
    def core(parity, counts, halo, blocks, partial, *refs):
        state, outs = refs[: state_size(index)], refs[state_size(index) :]
        for row in range(ROWS):
            raw = partial[row] + column_product(halo, blocks, row, 0)
            term, summed, msd = advance(index, coeffs, parity, counts, state, (0,), 0, row, raw)
            if index == TERMS - 1:
                outs[0][row, 0] = summed.astype(jnp.bfloat16)
                outs[1][row, 0] = msd
            else:
                outs[0][row, 0] = term.astype(jnp.bfloat16)
                outs[1][row, 0] = summed
                outs[2][row, 0] = term

    return core


def make_chip(index, coeffs):
    last = index == TERMS - 1

    def chip(parity, counts, halo, blocks, partial, inner, core, *refs):
        if last:
            inner_msd, core_msd = refs[:2]
            refs = refs[2:]
        state, outs = refs[: state_size(index)], refs[state_size(index) :]
        for row in range(ROWS):
            raw = partial[row] + column_product(halo, blocks, row, 3)
            term, summed, msd = advance(index, coeffs, parity, counts, state, (3,), 0, row, raw)
            if not last:
                message = outs[row]
                message[0] = core[row, 0]
                message[1] = inner[row, 0]
                message[2] = inner[row, 1]
                message[3] = term.astype(jnp.bfloat16)
                outs[2][row, 0] = summed
                outs[3][row, 0] = term
                continue
            displacements, msd_out = outs
            pieces = [core[row, 0], inner[row, 0], inner[row, 1], summed.astype(jnp.bfloat16)]
            means = [core_msd[row, 0], inner_msd[row, 0], inner_msd[row, 1], msd]
            for col in range(COLS):
                x, y = place(parity, row, col)
                displacements[x, y] = pieces[col]
            x, _ = place(parity, row, 0)
            msd_out[x] = jnp.where(
                parity[1] == 1, jnp.concatenate(means, axis=0), jnp.concatenate(means[::-1], axis=0)
            )

    return chip


def local(probes, counts, blocks):
    coeffs = chebyshev_weights(TERMS)
    x_index = lax.axis_index("gx")
    y_index = lax.axis_index("gy")
    parity = jnp.stack([x_index % 2, y_index % 2]).astype(jnp.int32)
    vmem = pl.BlockSpec(memory_space=pltpu.VMEM)
    smem = pl.BlockSpec(memory_space=pltpu.SMEM)
    hbm = pl.BlockSpec(memory_space=pl.ANY)
    dofs = probes.shape[3]
    count = probes.shape[2]
    cells = (COLS, count, dofs)
    raw = jax.ShapeDtypeStruct((ROWS, COLS, dofs, count), jnp.float32)
    rounded = jax.ShapeDtypeStruct(cells, jnp.bfloat16)
    params = pltpu.CompilerParams(vmem_limit_bytes=16 * 1024 * 1024)

    def cost(pairs):
        flops = 2 * pairs * count * dofs * dofs * 4
        return pl.CostEstimate(flops=flops, bytes_accessed=pairs * dofs * dofs * 2, transcendentals=0)

    def swap(value, axis, far):
        size = lax.axis_size(axis)
        if far:
            pairs = [(i, (i + 1) % size if i % 2 else (i - 1) % size) for i in range(size)]
        else:
            pairs = [(i, i ^ 1) for i in range(size)]
        return lax.ppermute(value, axis, pairs)

    far, near = pl.pallas_call(
        start_kernel,
        out_shape=(rounded, rounded),
        in_specs=[smem, smem, vmem],
        out_specs=(vmem, vmem),
        compiler_params=params,
        name="start",
    )(parity, counts, probes)
    start = [far, near]

    def column_state(cols, dtype):
        return jax.ShapeDtypeStruct((ROWS, cols, count, dofs), dtype)

    def run(body, operands, outs, pairs):
        return pl.pallas_call(
            body,
            out_shape=outs,
            in_specs=[smem, smem] + [vmem] * (len(operands) - 2),
            out_specs=tuple([vmem] * len(outs)),
            compiler_params=params,
            cost_estimate=cost(pairs),
        )(*operands)

    edge = jax.ShapeDtypeStruct((ROWS, dofs, count), jnp.float32)
    saved = {"inner": [], "core": [], "chip": []}
    held = None
    for index in range(1, TERMS):
        last = index == TERMS - 1
        halo_near = swap(near, "gx", False)
        halo_far = swap(far, "gx", True)
        if index == 1:
            held, partial = pl.pallas_call(
                load_kernel,
                out_shape=(pltpu.VMEM(blocks.shape, blocks.dtype), raw),
                in_specs=[smem, hbm, vmem, vmem],
                out_specs=(vmem, vmem),
                scratch_shapes=[pltpu.SemaphoreType.DMA((ROWS * COLS,))],
                compiler_params=params,
                cost_estimate=pl.CostEstimate(flops=0, bytes_accessed=blocks.size * 4, transcendentals=0),
                name="load",
            )(parity, blocks, far, near)
        else:
            partial = pl.pallas_call(
                own_kernel,
                out_shape=raw,
                in_specs=[vmem, vmem, vmem],
                out_specs=vmem,
                compiler_params=params,
                cost_estimate=cost(40),
                name="own",
            )(far, near, held)
        halo_far, halo_near, partial = lax.optimization_barrier((halo_far, halo_near, partial))
        core_edge, chip_edge = pl.pallas_call(
            edge_kernel,
            out_shape=(rounded, rounded),
            in_specs=[vmem] * 4,
            out_specs=(vmem, vmem),
            compiler_params=params,
            name="edges",
        )(halo_far, far, near, halo_near)
        halo_core = swap(core_edge, "gy", False)
        halo_chip = swap(chip_edge, "gy", True)

        def state(name, index=index, last=last):
            return saved[name] + (start if index <= 2 or last else [])

        def outputs(cols, last=last):
            if last:
                mean = jax.ShapeDtypeStruct((ROWS, cols, 1, dofs), jnp.float32)
                return (column_state(cols, jnp.bfloat16), mean)
            wide = column_state(cols, jnp.float32)
            return (column_state(cols, jnp.bfloat16), wide, wide)

        def keep(name, summed, term, index=index):
            terms[name].append(term)
            saved[name] = [summed] + ([terms[name][-2]] if index >= 2 else [])

        if index == 1:
            terms = {"inner": [], "core": [], "chip": []}
        fixed = [parity, counts]
        core_raw, chip_raw, inner, *rest = run(
            make_rows(index, coeffs),
            fixed + [halo_far, halo_near, held, partial] + state("inner"),
            (edge, edge) + outputs(2),
            20,
        )
        core, *core_rest = run(
            make_core(index, coeffs),
            fixed + [halo_core, held, core_raw] + state("core"),
            outputs(1),
            6,
        )
        operands = fixed + [halo_chip, held, chip_raw, inner, core]
        if last:
            operands += [rest[0], core_rest[0]]
            outs = (
                jax.ShapeDtypeStruct(probes.shape, jnp.bfloat16),
                jax.ShapeDtypeStruct((ROWS, COLS, dofs), jnp.float32),
            )
        else:
            wide = column_state(1, jnp.float32)
            outs = (rounded, rounded, wide, wide)
        results = run(make_chip(index, coeffs), operands + state("chip"), outs, 6)
        if not last:
            far, near = results[:2]
            keep("inner", *rest)
            keep("core", *core_rest)
            keep("chip", *results[2:])
    return tuple(results)


def solution(mesh):
    return jax.shard_map(
        local,
        mesh=mesh,
        in_specs=(P("gx", "gy", None, None), P("gx", "gy"), P("gx", "gy", None, None, None)),
        out_specs=(P("gx", "gy", None, None), P("gx", "gy", None)),
        check_vma=False,
    )
```

profile of v0, /device:TPU:97, one launch (start us, length us, event | category | flops | bytes accessed | tf_op | source)
XLA Modules:
  0.0 160.9 jit_solution(2603482906228010064)
XLA Ops:
  3.0 5.2 %collective-permute-start = (bf16[4,64,384]{2,1,0:T(8,128)(2,1)S(1)}, bf16[4,64,384]{2,1,0:T(8,128)(2,1)S(1)}, u32[]{:S(2)}, u32[]{:S(2)}) collective-permute-start(bf16[4,64,384]{2,1,0:T(8,128)(2,1)S(1)} %get-tuple-element.116.far.refs_0_.refs_1_.refs_2_.refs_4_), channel_id=1, source_target_pairs={{0,112},{16,32},{32,16},{48,64},{64,48},{80,96},{96,80},{112,0},{1... | collective-permute-start | bytes 589832 | tf_op jit(solution)/shard_map/ppermute | solution.py:253
  8.2 9.5 %load.1 = (bf16[2,4,9,384,384]{4,3,2,1,0:T(8,128)(2,1)S(1)}, f32[2,4,384,64]{3,2,1,0:T(8,128)S(1)}) custom-call(s32[2]{0:T(128)S(1)} %pad_add_fusion.parity, bf16[2,4,9,384,384]{4,3,2,1,0:T(8,128)(2,1)} %blocks.1, bf16[4,64,384]{2,1,0:T(8,128)(2,1)S(1)} %get-tuple-element.116.far.refs_0_.refs_1_.refs_2_.refs_4_, ...), custom_call_target="tpu_custom_call" | custom-call | bytes 42467328 | tf_op jit(solution)/shard_map/load/pallas_call | solution.py:286
  22.3 3.7 %collective-permute-done.2.halo = bf16[4,64,384]{2,1,0:T(8,128)(2,1)S(1)} collective-permute-done((bf16[4,64,384]{2,1,0:T(8,128)(2,1)S(1)}, bf16[4,64,384]{2,1,0:T(8,128)(2,1)S(1)}, u32[]{:S(2)}, u32[]{:S(2)}) %collective-permute-start.2) | collective-permute-done | bytes 196640 | tf_op jit(solution)/shard_map/ppermute | solution.py:253
  27.3 3.6 %collective-permute-start.4 = (bf16[4,64,384]{2,1,0:T(8,128)(2,1)S(1)}, bf16[4,64,384]{2,1,0:T(8,128)(2,1)S(1)}, u32[]{:S(2)}, u32[]{:S(2)}) collective-permute-start(bf16[4,64,384]{2,1,0:T(8,128)(2,1)S(1)} %get-tuple-element.129.far), channel_id=1, source_target_pairs={{0,112},{16,32},{32,16},{48,64},{64,48},{80,96},{96,80},{112,0},{1... | collective-permute-start | bytes 589832 | tf_op jit(solution)/shard_map/ppermute | solution.py:253
  30.9 3.2 %own.6.partial = f32[2,4,384,64]{3,2,1,0:T(8,128)S(1)} custom-call(bf16[4,64,384]{2,1,0:T(8,128)(2,1)S(1)} %get-tuple-element.129.far, bf16[4,64,384]{2,1,0:T(8,128)(2,1)S(1)} %get-tuple-element.130.near, bf16[2,4,9,384,384]{4,3,2,1,0:T(8,128)(2,1)S(1)} %get-tuple-element.122.blocks), custom_call_target="tpu_custom_call" | custom-call | flops 3019898880 | bytes 11796480 | tf_op jit(solution)/shard_map/own/pallas_call | solution.py:297
  36.1 4.3 %collective-permute-done.5.halo_near = bf16[4,64,384]{2,1,0:T(8,128)(2,1)S(1)} collective-permute-done((bf16[4,64,384]{2,1,0:T(8,128)(2,1)S(1)}, bf16[4,64,384]{2,1,0:T(8,128)(2,1)S(1)}, u32[]{:S(2)}, u32[]{:S(2)}) %collective-permute-start.5) | collective-permute-done | bytes 196640 | tf_op jit(solution)/shard_map/ppermute | solution.py:253
  44.5 3.7 %collective-permute-done.6.halo = bf16[4,64,384]{2,1,0:T(8,128)(2,1)S(1)} collective-permute-done((bf16[4,64,384]{2,1,0:T(8,128)(2,1)S(1)}, bf16[4,64,384]{2,1,0:T(8,128)(2,1)S(1)}, u32[]{:S(2)}, u32[]{:S(2)}) %collective-permute-start.6) | collective-permute-done | bytes 196640 | tf_op jit(solution)/shard_map/ppermute | solution.py:253
  52.5 3.2 %own.7.partial = f32[2,4,384,64]{3,2,1,0:T(8,128)S(1)} custom-call(bf16[4,64,384]{2,1,0:T(8,128)(2,1)S(1)} %get-tuple-element.143.far, bf16[4,64,384]{2,1,0:T(8,128)(2,1)S(1)} %get-tuple-element.144.near, bf16[2,4,9,384,384]{4,3,2,1,0:T(8,128)(2,1)S(1)} %get-tuple-element.122.blocks), custom_call_target="tpu_custom_call" | custom-call | flops 3019898880 | bytes 11796480 | tf_op jit(solution)/shard_map/own/pallas_call | solution.py:297
  58.3 4.3 %collective-permute-done.9.halo_near = bf16[4,64,384]{2,1,0:T(8,128)(2,1)S(1)} collective-permute-done((bf16[4,64,384]{2,1,0:T(8,128)(2,1)S(1)}, bf16[4,64,384]{2,1,0:T(8,128)(2,1)S(1)}, u32[]{:S(2)}, u32[]{:S(2)}) %collective-permute-start.9) | collective-permute-done | bytes 196640 | tf_op jit(solution)/shard_map/ppermute | solution.py:253
  66.6 3.7 %collective-permute-done.10.halo = bf16[4,64,384]{2,1,0:T(8,128)(2,1)S(1)} collective-permute-done((bf16[4,64,384]{2,1,0:T(8,128)(2,1)S(1)}, bf16[4,64,384]{2,1,0:T(8,128)(2,1)S(1)}, u32[]{:S(2)}, u32[]{:S(2)}) %collective-permute-start.10) | collective-permute-done | bytes 196640 | tf_op jit(solution)/shard_map/ppermute | solution.py:253
  71.5 5.4 %collective-permute-start.12 = (bf16[4,64,384]{2,1,0:T(8,128)(2,1)S(1)}, bf16[4,64,384]{2,1,0:T(8,128)(2,1)S(1)}, u32[]{:S(2)}, u32[]{:S(2)}) collective-permute-start(bf16[4,64,384]{2,1,0:T(8,128)(2,1)S(1)} %get-tuple-element.160.far), channel_id=1, source_target_pairs={{0,112},{16,32},{32,16},{48,64},{64,48},{80,96},{96,80},{112,0},{1... | collective-permute-start | bytes 589832 | tf_op jit(solution)/shard_map/ppermute | solution.py:253
  80.4 4.1 %collective-permute-done.13.halo_near = bf16[4,64,384]{2,1,0:T(8,128)(2,1)S(1)} collective-permute-done((bf16[4,64,384]{2,1,0:T(8,128)(2,1)S(1)}, bf16[4,64,384]{2,1,0:T(8,128)(2,1)S(1)}, u32[]{:S(2)}, u32[]{:S(2)}) %collective-permute-start.13) | collective-permute-done | bytes 196640 | tf_op jit(solution)/shard_map/ppermute | solution.py:253
  88.3 3.7 %collective-permute-done.14.halo = bf16[4,64,384]{2,1,0:T(8,128)(2,1)S(1)} collective-permute-done((bf16[4,64,384]{2,1,0:T(8,128)(2,1)S(1)}, bf16[4,64,384]{2,1,0:T(8,128)(2,1)S(1)}, u32[]{:S(2)}, u32[]{:S(2)}) %collective-permute-start.14) | collective-permute-done | bytes 196640 | tf_op jit(solution)/shard_map/ppermute | solution.py:253
  93.2 6.3 %collective-permute-start.16 = (bf16[4,64,384]{2,1,0:T(8,128)(2,1)S(1)}, bf16[4,64,384]{2,1,0:T(8,128)(2,1)S(1)}, u32[]{:S(2)}, u32[]{:S(2)}) collective-permute-start(bf16[4,64,384]{2,1,0:T(8,128)(2,1)S(1)} %get-tuple-element.177.far), channel_id=1, source_target_pairs={{0,112},{16,32},{32,16},{48,64},{64,48},{80,96},{96,80},{112,0},{1... | collective-permute-start | bytes 589832 | tf_op jit(solution)/shard_map/ppermute | solution.py:253
  99.6 3.2 %own.9.partial = f32[2,4,384,64]{3,2,1,0:T(8,128)S(1)} custom-call(bf16[4,64,384]{2,1,0:T(8,128)(2,1)S(1)} %get-tuple-element.177.far, bf16[4,64,384]{2,1,0:T(8,128)(2,1)S(1)} %get-tuple-element.178.near, bf16[2,4,9,384,384]{4,3,2,1,0:T(8,128)(2,1)S(1)} %get-tuple-element.122.blocks), custom_call_target="tpu_custom_call" | custom-call | flops 3019898880 | bytes 11796480 | tf_op jit(solution)/shard_map/own/pallas_call | solution.py:297
  102.8 3.8 %collective-permute-done.17.halo_near = bf16[4,64,384]{2,1,0:T(8,128)(2,1)S(1)} collective-permute-done((bf16[4,64,384]{2,1,0:T(8,128)(2,1)S(1)}, bf16[4,64,384]{2,1,0:T(8,128)(2,1)S(1)}, u32[]{:S(2)}, u32[]{:S(2)}) %collective-permute-start.17) | collective-permute-done | bytes 196640 | tf_op jit(solution)/shard_map/ppermute | solution.py:253
  110.5 3.7 %collective-permute-done.18.halo = bf16[4,64,384]{2,1,0:T(8,128)(2,1)S(1)} collective-permute-done((bf16[4,64,384]{2,1,0:T(8,128)(2,1)S(1)}, bf16[4,64,384]{2,1,0:T(8,128)(2,1)S(1)}, u32[]{:S(2)}, u32[]{:S(2)}) %collective-permute-start.18) | collective-permute-done | bytes 196640 | tf_op jit(solution)/shard_map/ppermute | solution.py:253
  115.4 5.7 %collective-permute-start.20 = (bf16[4,64,384]{2,1,0:T(8,128)(2,1)S(1)}, bf16[4,64,384]{2,1,0:T(8,128)(2,1)S(1)}, u32[]{:S(2)}, u32[]{:S(2)}) collective-permute-start(bf16[4,64,384]{2,1,0:T(8,128)(2,1)S(1)} %get-tuple-element.194.far), channel_id=1, source_target_pairs={{0,112},{16,32},{32,16},{48,64},{64,48},{80,96},{96,80},{112,0},{1... | collective-permute-start | bytes 589832 | tf_op jit(solution)/shard_map/ppermute | solution.py:253
  121.1 3.2 %own.10.partial = f32[2,4,384,64]{3,2,1,0:T(8,128)S(1)} custom-call(bf16[4,64,384]{2,1,0:T(8,128)(2,1)S(1)} %get-tuple-element.194.far, bf16[4,64,384]{2,1,0:T(8,128)(2,1)S(1)} %get-tuple-element.195.near, bf16[2,4,9,384,384]{4,3,2,1,0:T(8,128)(2,1)S(1)} %get-tuple-element.122.blocks), custom_call_target="tpu_custom_call" | custom-call | flops 3019898880 | bytes 11796480 | tf_op jit(solution)/shard_map/own/pallas_call | solution.py:297
  124.4 4.1 %collective-permute-done.21.halo_near = bf16[4,64,384]{2,1,0:T(8,128)(2,1)S(1)} collective-permute-done((bf16[4,64,384]{2,1,0:T(8,128)(2,1)S(1)}, bf16[4,64,384]{2,1,0:T(8,128)(2,1)S(1)}, u32[]{:S(2)}, u32[]{:S(2)}) %collective-permute-start.21) | collective-permute-done | bytes 196640 | tf_op jit(solution)/shard_map/ppermute | solution.py:253
  137.8 3.4 %collective-permute-start.24 = (bf16[4,64,384]{2,1,0:T(8,128)(2,1)S(1)}, bf16[4,64,384]{2,1,0:T(8,128)(2,1)S(1)}, u32[]{:S(2)}, u32[]{:S(2)}) collective-permute-start(bf16[4,64,384]{2,1,0:T(8,128)(2,1)S(1)} %get-tuple-element.211.far), channel_id=1, source_target_pairs={{0,112},{16,32},{32,16},{48,64},{64,48},{80,96},{96,80},{112,0},{1... | collective-permute-start | bytes 589832 | tf_op jit(solution)/shard_map/ppermute | solution.py:253
  141.2 3.2 %own.11.partial = f32[2,4,384,64]{3,2,1,0:T(8,128)S(1)} custom-call(bf16[4,64,384]{2,1,0:T(8,128)(2,1)S(1)} %get-tuple-element.211.far, bf16[4,64,384]{2,1,0:T(8,128)(2,1)S(1)} %get-tuple-element.212.near, bf16[2,4,9,384,384]{4,3,2,1,0:T(8,128)(2,1)S(1)} %get-tuple-element.122.blocks), custom_call_target="tpu_custom_call" | custom-call | flops 3019898880 | bytes 11796480 | tf_op jit(solution)/shard_map/own/pallas_call | solution.py:297
  146.9 4.3 %collective-permute-done.25.halo_near = bf16[4,64,384]{2,1,0:T(8,128)(2,1)S(1)} collective-permute-done((bf16[4,64,384]{2,1,0:T(8,128)(2,1)S(1)}, bf16[4,64,384]{2,1,0:T(8,128)(2,1)S(1)}, u32[]{:S(2)}, u32[]{:S(2)}) %collective-permute-start.25) | collective-permute-done | bytes 196640 | tf_op jit(solution)/shard_map/ppermute | solution.py:253
  155.4 3.5 %collective-permute-done.26.halo = bf16[4,64,384]{2,1,0:T(8,128)(2,1)S(1)} collective-permute-done((bf16[4,64,384]{2,1,0:T(8,128)(2,1)S(1)}, bf16[4,64,384]{2,1,0:T(8,128)(2,1)S(1)}, u32[]{:S(2)}, u32[]{:S(2)}) %collective-permute-start.26) | collective-permute-done | bytes 196640 | tf_op jit(solution)/shard_map/ppermute | solution.py:253
  (73 shorter events, 58.0 us)
Async XLA Ops:
  3.0 14.7 %collective-permute-start = (bf16[4,64,384]{2,1,0:T(8,128)(2,1)S(1)}, bf16[4,64,384]{2,1,0:T(8,128)(2,1)S(1)}, u32[]{:S(2)}, u32[]{:S(2)}) collective-permute-start(bf16[4,64,384]{2,1,0:T(8,128)(2,1)S(1)} %get-tuple-element.116.far.refs_0_.refs_1_.refs_2_.refs_4_), channel_id=1, source_target_pairs={{0,112},{16,32},{32,16},{48,64},{64,48},{80,96},{96,80},{112,0},{1... | collective-permute-start | bytes 589832 | tf_op jit(solution)/shard_map/ppermute | solution.py:253
  8.2 9.5 %collective-permute-start.1 = (bf16[4,64,384]{2,1,0:T(8,128)(2,1)S(1)}, bf16[4,64,384]{2,1,0:T(8,128)(2,1)S(1)}, u32[]{:S(2)}, u32[]{:S(2)}) collective-permute-start(bf16[4,64,384]{2,1,0:T(8,128)(2,1)S(1)} %get-tuple-element.117.near.refs_1_.refs_2_.refs_3_.refs_5_), channel_id=1, source_target_pairs={{0,16},{16,0},{32,48},{48,32},{64,80},{80,64},{96,112},{112,96},{1... | collective-permute-start | bytes 589832 | tf_op jit(solution)/shard_map/ppermute | solution.py:253
  17.8 3.3 %collective-permute-start.3 = (bf16[4,64,384]{2,1,0:T(8,128)(2,1)S(1)}, bf16[4,64,384]{2,1,0:T(8,128)(2,1)S(1)}, u32[]{:S(2)}, u32[]{:S(2)}) collective-permute-start(bf16[4,64,384]{2,1,0:T(8,128)(2,1)S(1)} %get-tuple-element.126), channel_id=1, source_target_pairs={{0,1},{1,0},{2,3},{3,2},{4,5},{5,4},{6,7},{7,6},{8,9},{9,8},{10,11... | collective-permute-start | bytes 589832 | tf_op jit(solution)/shard_map/ppermute | solution.py:253
  18.8 7.2 %collective-permute-start.2 = (bf16[4,64,384]{2,1,0:T(8,128)(2,1)S(1)}, bf16[4,64,384]{2,1,0:T(8,128)(2,1)S(1)}, u32[]{:S(2)}, u32[]{:S(2)}) collective-permute-start(bf16[4,64,384]{2,1,0:T(8,128)(2,1)S(1)} %get-tuple-element.121), channel_id=1, source_target_pairs={{0,15},{1,2},{2,1},{3,4},{4,3},{5,6},{6,5},{7,8},{8,7},{9,10},{10,... | collective-permute-start | bytes 589832 | tf_op jit(solution)/shard_map/ppermute | solution.py:253
  27.3 8.9 %collective-permute-start.4 = (bf16[4,64,384]{2,1,0:T(8,128)(2,1)S(1)}, bf16[4,64,384]{2,1,0:T(8,128)(2,1)S(1)}, u32[]{:S(2)}, u32[]{:S(2)}) collective-permute-start(bf16[4,64,384]{2,1,0:T(8,128)(2,1)S(1)} %get-tuple-element.129.far), channel_id=1, source_target_pairs={{0,112},{16,32},{32,16},{48,64},{64,48},{80,96},{96,80},{112,0},{1... | collective-permute-start | bytes 589832 | tf_op jit(solution)/shard_map/ppermute | solution.py:253
  30.9 9.6 %collective-permute-start.5 = (bf16[4,64,384]{2,1,0:T(8,128)(2,1)S(1)}, bf16[4,64,384]{2,1,0:T(8,128)(2,1)S(1)}, u32[]{:S(2)}, u32[]{:S(2)}) collective-permute-start(bf16[4,64,384]{2,1,0:T(8,128)(2,1)S(1)} %get-tuple-element.130.near), channel_id=1, source_target_pairs={{0,16},{16,0},{32,48},{48,32},{64,80},{80,64},{96,112},{112,96},{1... | collective-permute-start | bytes 589832 | tf_op jit(solution)/shard_map/ppermute | solution.py:253
  41.0 7.2 %collective-permute-start.6 = (bf16[4,64,384]{2,1,0:T(8,128)(2,1)S(1)}, bf16[4,64,384]{2,1,0:T(8,128)(2,1)S(1)}, u32[]{:S(2)}, u32[]{:S(2)}) collective-permute-start(bf16[4,64,384]{2,1,0:T(8,128)(2,1)S(1)} %get-tuple-element.133), channel_id=1, source_target_pairs={{0,15},{1,2},{2,1},{3,4},{4,3},{5,6},{6,5},{7,8},{8,7},{9,10},{10,... | collective-permute-start | bytes 589832 | tf_op jit(solution)/shard_map/ppermute | solution.py:253
  49.4 8.9 %collective-permute-start.8 = (bf16[4,64,384]{2,1,0:T(8,128)(2,1)S(1)}, bf16[4,64,384]{2,1,0:T(8,128)(2,1)S(1)}, u32[]{:S(2)}, u32[]{:S(2)}) collective-permute-start(bf16[4,64,384]{2,1,0:T(8,128)(2,1)S(1)} %get-tuple-element.143.far), channel_id=1, source_target_pairs={{0,112},{16,32},{32,16},{48,64},{64,48},{80,96},{96,80},{112,0},{1... | collective-permute-start | bytes 589832 | tf_op jit(solution)/shard_map/ppermute | solution.py:253
  52.5 10.1 %collective-permute-start.9 = (bf16[4,64,384]{2,1,0:T(8,128)(2,1)S(1)}, bf16[4,64,384]{2,1,0:T(8,128)(2,1)S(1)}, u32[]{:S(2)}, u32[]{:S(2)}) collective-permute-start(bf16[4,64,384]{2,1,0:T(8,128)(2,1)S(1)} %get-tuple-element.144.near), channel_id=1, source_target_pairs={{0,16},{16,0},{32,48},{48,32},{64,80},{80,64},{96,112},{112,96},{1... | collective-permute-start | bytes 589832 | tf_op jit(solution)/shard_map/ppermute | solution.py:253
  63.1 7.2 %collective-permute-start.10 = (bf16[4,64,384]{2,1,0:T(8,128)(2,1)S(1)}, bf16[4,64,384]{2,1,0:T(8,128)(2,1)S(1)}, u32[]{:S(2)}, u32[]{:S(2)}) collective-permute-start(bf16[4,64,384]{2,1,0:T(8,128)(2,1)S(1)} %get-tuple-element.147), channel_id=1, source_target_pairs={{0,15},{1,2},{2,1},{3,4},{4,3},{5,6},{6,5},{7,8},{8,7},{9,10},{10,... | collective-permute-start | bytes 589832 | tf_op jit(solution)/shard_map/ppermute | solution.py:253
  71.5 8.9 %collective-permute-start.12 = (bf16[4,64,384]{2,1,0:T(8,128)(2,1)S(1)}, bf16[4,64,384]{2,1,0:T(8,128)(2,1)S(1)}, u32[]{:S(2)}, u32[]{:S(2)}) collective-permute-start(bf16[4,64,384]{2,1,0:T(8,128)(2,1)S(1)} %get-tuple-element.160.far), channel_id=1, source_target_pairs={{0,112},{16,32},{32,16},{48,64},{64,48},{80,96},{96,80},{112,0},{1... | collective-permute-start | bytes 589832 | tf_op jit(solution)/shard_map/ppermute | solution.py:253
  77.0 7.6 %collective-permute-start.13 = (bf16[4,64,384]{2,1,0:T(8,128)(2,1)S(1)}, bf16[4,64,384]{2,1,0:T(8,128)(2,1)S(1)}, u32[]{:S(2)}, u32[]{:S(2)}) collective-permute-start(bf16[4,64,384]{2,1,0:T(8,128)(2,1)S(1)} %get-tuple-element.161.near), channel_id=1, source_target_pairs={{0,16},{16,0},{32,48},{48,32},{64,80},{80,64},{96,112},{112,96},{1... | collective-permute-start | bytes 589832 | tf_op jit(solution)/shard_map/ppermute | solution.py:253
  84.8 7.2 %collective-permute-start.14 = (bf16[4,64,384]{2,1,0:T(8,128)(2,1)S(1)}, bf16[4,64,384]{2,1,0:T(8,128)(2,1)S(1)}, u32[]{:S(2)}, u32[]{:S(2)}) collective-permute-start(bf16[4,64,384]{2,1,0:T(8,128)(2,1)S(1)} %get-tuple-element.164), channel_id=1, source_target_pairs={{0,15},{1,2},{2,1},{3,4},{4,3},{5,6},{6,5},{7,8},{8,7},{9,10},{10,... | collective-permute-start | bytes 589832 | tf_op jit(solution)/shard_map/ppermute | solution.py:253
  93.2 9.5 %collective-permute-start.16 = (bf16[4,64,384]{2,1,0:T(8,128)(2,1)S(1)}, bf16[4,64,384]{2,1,0:T(8,128)(2,1)S(1)}, u32[]{:S(2)}, u32[]{:S(2)}) collective-permute-start(bf16[4,64,384]{2,1,0:T(8,128)(2,1)S(1)} %get-tuple-element.177.far), channel_id=1, source_target_pairs={{0,112},{16,32},{32,16},{48,64},{64,48},{80,96},{96,80},{112,0},{1... | collective-permute-start | bytes 589832 | tf_op jit(solution)/shard_map/ppermute | solution.py:253
  99.6 6.9 %collective-permute-start.17 = (bf16[4,64,384]{2,1,0:T(8,128)(2,1)S(1)}, bf16[4,64,384]{2,1,0:T(8,128)(2,1)S(1)}, u32[]{:S(2)}, u32[]{:S(2)}) collective-permute-start(bf16[4,64,384]{2,1,0:T(8,128)(2,1)S(1)} %get-tuple-element.178.near), channel_id=1, source_target_pairs={{0,16},{16,0},{32,48},{48,32},{64,80},{80,64},{96,112},{112,96},{1... | collective-permute-start | bytes 589832 | tf_op jit(solution)/shard_map/ppermute | solution.py:253
  106.6 7.5 %collective-permute-start.18 = (bf16[4,64,384]{2,1,0:T(8,128)(2,1)S(1)}, bf16[4,64,384]{2,1,0:T(8,128)(2,1)S(1)}, u32[]{:S(2)}, u32[]{:S(2)}) collective-permute-start(bf16[4,64,384]{2,1,0:T(8,128)(2,1)S(1)} %get-tuple-element.181), channel_id=1, source_target_pairs={{0,15},{1,2},{2,1},{3,4},{4,3},{5,6},{6,5},{7,8},{8,7},{9,10},{10,... | collective-permute-start | bytes 589832 | tf_op jit(solution)/shard_map/ppermute | solution.py:253
  115.4 9.0 %collective-permute-start.20 = (bf16[4,64,384]{2,1,0:T(8,128)(2,1)S(1)}, bf16[4,64,384]{2,1,0:T(8,128)(2,1)S(1)}, u32[]{:S(2)}, u32[]{:S(2)}) collective-permute-start(bf16[4,64,384]{2,1,0:T(8,128)(2,1)S(1)} %get-tuple-element.194.far), channel_id=1, source_target_pairs={{0,112},{16,32},{32,16},{48,64},{64,48},{80,96},{96,80},{112,0},{1... | collective-permute-start | bytes 589832 | tf_op jit(solution)/shard_map/ppermute | solution.py:253
  121.1 7.4 %collective-permute-start.21 = (bf16[4,64,384]{2,1,0:T(8,128)(2,1)S(1)}, bf16[4,64,384]{2,1,0:T(8,128)(2,1)S(1)}, u32[]{:S(2)}, u32[]{:S(2)}) collective-permute-start(bf16[4,64,384]{2,1,0:T(8,128)(2,1)S(1)} %get-tuple-element.195.near), channel_id=1, source_target_pairs={{0,16},{16,0},{32,48},{48,32},{64,80},{80,64},{96,112},{112,96},{1... | collective-permute-start | bytes 589832 | tf_op jit(solution)/shard_map/ppermute | solution.py:253
  128.5 3.2 %collective-permute-start.23 = (bf16[4,64,384]{2,1,0:T(8,128)(2,1)S(1)}, bf16[4,64,384]{2,1,0:T(8,128)(2,1)S(1)}, u32[]{:S(2)}, u32[]{:S(2)}) collective-permute-start(bf16[4,64,384]{2,1,0:T(8,128)(2,1)S(1)} %get-tuple-element.204), channel_id=1, source_target_pairs={{0,1},{1,0},{2,3},{3,2},{4,5},{5,4},{6,7},{7,6},{8,9},{9,8},{10,11... | collective-permute-start | bytes 589832 | tf_op jit(solution)/shard_map/ppermute | solution.py:253
  128.6 7.3 %collective-permute-start.22 = (bf16[4,64,384]{2,1,0:T(8,128)(2,1)S(1)}, bf16[4,64,384]{2,1,0:T(8,128)(2,1)S(1)}, u32[]{:S(2)}, u32[]{:S(2)}) collective-permute-start(bf16[4,64,384]{2,1,0:T(8,128)(2,1)S(1)} %get-tuple-element.198), channel_id=1, source_target_pairs={{0,15},{1,2},{2,1},{3,4},{4,3},{5,6},{6,5},{7,8},{8,7},{9,10},{10,... | collective-permute-start | bytes 589832 | tf_op jit(solution)/shard_map/ppermute | solution.py:253
  137.8 9.1 %collective-permute-start.24 = (bf16[4,64,384]{2,1,0:T(8,128)(2,1)S(1)}, bf16[4,64,384]{2,1,0:T(8,128)(2,1)S(1)}, u32[]{:S(2)}, u32[]{:S(2)}) collective-permute-start(bf16[4,64,384]{2,1,0:T(8,128)(2,1)S(1)} %get-tuple-element.211.far), channel_id=1, source_target_pairs={{0,112},{16,32},{32,16},{48,64},{64,48},{80,96},{96,80},{112,0},{1... | collective-permute-start | bytes 589832 | tf_op jit(solution)/shard_map/ppermute | solution.py:253
  141.2 10.0 %collective-permute-start.25 = (bf16[4,64,384]{2,1,0:T(8,128)(2,1)S(1)}, bf16[4,64,384]{2,1,0:T(8,128)(2,1)S(1)}, u32[]{:S(2)}, u32[]{:S(2)}) collective-permute-start(bf16[4,64,384]{2,1,0:T(8,128)(2,1)S(1)} %get-tuple-element.212.near), channel_id=1, source_target_pairs={{0,16},{16,0},{32,48},{48,32},{64,80},{80,64},{96,112},{112,96},{1... | collective-permute-start | bytes 589832 | tf_op jit(solution)/shard_map/ppermute | solution.py:253
  151.2 2.9 %collective-permute-start.27 = (bf16[4,64,384]{2,1,0:T(8,128)(2,1)S(1)}, bf16[4,64,384]{2,1,0:T(8,128)(2,1)S(1)}, u32[]{:S(2)}, u32[]{:S(2)}) collective-permute-start(bf16[4,64,384]{2,1,0:T(8,128)(2,1)S(1)} %get-tuple-element.221), channel_id=1, source_target_pairs={{0,1},{1,0},{2,3},{3,2},{4,5},{5,4},{6,7},{7,6},{8,9},{9,8},{10,11... | collective-permute-start | bytes 589832 | tf_op jit(solution)/shard_map/ppermute | solution.py:253
  151.7 7.2 %collective-permute-start.26 = (bf16[4,64,384]{2,1,0:T(8,128)(2,1)S(1)}, bf16[4,64,384]{2,1,0:T(8,128)(2,1)S(1)}, u32[]{:S(2)}, u32[]{:S(2)}) collective-permute-start(bf16[4,64,384]{2,1,0:T(8,128)(2,1)S(1)} %get-tuple-element.215), channel_id=1, source_target_pairs={{0,15},{1,2},{2,1},{3,4},{4,3},{5,6},{6,5},{7,8},{8,7},{9,10},{10,... | collective-permute-start | bytes 589832 | tf_op jit(solution)/shard_map/ppermute | solution.py:253
  (6 other events, 12.3 us)
where the time goes:
time: 164 us; the launch traced here: 161 us
  Pallas kernels  65.3 us (40%)
  waiting for transfers between devices  56.8 us (35%)
  starting transfers between devices  36.1 us (22%)
  local copies, waits for them, and re-layouts  1.67 us (1%)
    ppermute x28, waiting for transfers between devices, swap(): return lax.ppermute(value, axis, pairs)  56.8 us
    ppermute x28, starting transfers between devices, swap(): return lax.ppermute(value, axis, pairs)  36.1 us
    pallas_call x21, Pallas kernels, run(): pl.pallas_call(body, out_shape=outs, in_specs=[smem, smem] + [vmem] * (le...  35.9 us
    pallas_call x6, Pallas kernels, local(): pl.pallas_call(own_kernel, out_shape=raw, in_specs=[vmem, vmem, vmem], ou...  19.1 us
    pallas_call x1, Pallas kernels, local(): pl.pallas_call(load_kernel, out_shape=(pltpu.VMEM(blocks.shape, blocks.dt...  9.49 us
  transfers between devices with their start and end apart: 28, of which 18 were waited for; matrix products, arithmetic and copies ran while one was open for 0% of the time, Pallas kernels for 34%

commit v1 on v0

--- a/solution.py
+++ b/solution.py
@@ -58,18 +58,23 @@
     return 3 * dx + dy
 
 
-def start_kernel(parity, counts, probes, far, near):
-    lane = lax.broadcasted_iota(jnp.int32, probes.shape[2:], 1)
+def start_kernel(parity, counts, probes, far, near, mask):
+    lane = lax.broadcasted_iota(jnp.int32, (1, probes.shape[3]), 1)
     for row, out in enumerate((far, near)):
         for col in range(COLS):
             x, y = place(parity, row, col)
-            live = lane < 3 * counts[x, y]
-            out[col] = jnp.where(live, probes[x, y].astype(jnp.float32), 0.0).astype(jnp.bfloat16)
+            live = jnp.where(lane < 3 * counts[x, y], 1.0, 0.0)
+            mask[row, col] = live
+            out[col] = (probes[x, y].astype(jnp.float32) * live).astype(jnp.bfloat16)
+
+
+AHEAD = 3
 
 
 def load_kernel(parity, blocks, far, near, out, total, sems):
     cells = [(row, col) for row in range(ROWS) for col in range(COLS)]
-    for row, col in cells:
+
+    def begin(row, col):
         x, y = place(parity, row, col)
         for step_row in range(3):
             for step_col in range(3):
@@ -78,7 +83,12 @@
                     out.at[row, col, 3 * step_row + step_col],
                     sems.at[COLS * row + col],
                 ).start()
-    for row, col in cells:
+
+    for cell in cells[:AHEAD]:
+        begin(*cell)
+    for number, (row, col) in enumerate(cells):
+        if number + AHEAD < len(cells):
+            begin(*cells[number + AHEAD])
         pltpu.make_async_copy(blocks.at[row, col], out.at[row, col], sems.at[COLS * row + col]).wait()
         total[row, col] = own_product(far, near, out, row, col)
 
@@ -126,11 +136,9 @@
         chip_edge[slot] = ref[COLS - 1]
 
 
-def advance(index, coeffs, parity, counts, state, cols, slot, row, raw):
+def advance(index, coeffs, mask, state, cols, slot, row, raw):
     col = cols[slot]
-    x, y = place(parity, row, col)
-    lane = lax.broadcasted_iota(jnp.int32, raw.shape[::-1], 1)
-    applied = jnp.where(lane < 3 * counts[x, y], raw.T, 0.0)
+    applied = jnp.where(mask[row, col] > 0.0, raw.T, 0.0)
     first = None
     if index in (1, 2, TERMS - 1):
         first = state[-2:][row][col].astype(jnp.float32)
@@ -153,7 +161,7 @@
 
 
 def make_rows(index, coeffs):
-    def rows(parity, counts, halo_far, halo_near, blocks, partial, *refs):
+    def rows(mask, halo_far, halo_near, blocks, partial, *refs):
         state, outs = refs[: state_size(index)], refs[state_size(index) :]
         for row, ref in enumerate((halo_far, halo_near)):
             for col in (1, 2, 0, 3):
@@ -162,31 +170,33 @@
                     outs[0 if col == 0 else 1][row] = raw
                     continue
                 slot = col - 1
-                term, summed, msd = advance(index, coeffs, parity, counts, state, (1, 2), slot, row, raw)
+                term, summed, msd = advance(index, coeffs, mask, state, (1, 2), slot, row, raw)
                 if index == TERMS - 1:
                     outs[2][row, slot] = summed.astype(jnp.bfloat16)
                     outs[3][row, slot] = msd
                 else:
                     outs[2][row, slot] = term.astype(jnp.bfloat16)
                     outs[3][row, slot] = summed
-                    outs[4][row, slot] = term
+                    if index < TERMS - 2:
+                        outs[4][row, slot] = term
 
     return rows
 
 
 def make_core(index, coeffs):
-    def core(parity, counts, halo, blocks, partial, *refs):
+    def core(mask, halo, blocks, partial, *refs):
         state, outs = refs[: state_size(index)], refs[state_size(index) :]
         for row in range(ROWS):
             raw = partial[row] + column_product(halo, blocks, row, 0)
-            term, summed, msd = advance(index, coeffs, parity, counts, state, (0,), 0, row, raw)
+            term, summed, msd = advance(index, coeffs, mask, state, (0,), 0, row, raw)
             if index == TERMS - 1:
                 outs[0][row, 0] = summed.astype(jnp.bfloat16)
                 outs[1][row, 0] = msd
             else:
                 outs[0][row, 0] = term.astype(jnp.bfloat16)
                 outs[1][row, 0] = summed
-                outs[2][row, 0] = term
+                if index < TERMS - 2:
+                    outs[2][row, 0] = term
 
     return core
 
@@ -194,14 +204,14 @@
 def make_chip(index, coeffs):
     last = index == TERMS - 1
 
-    def chip(parity, counts, halo, blocks, partial, inner, core, *refs):
+    def chip(mask, halo, blocks, partial, inner, core, *refs):
         if last:
-            inner_msd, core_msd = refs[:2]
-            refs = refs[2:]
+            parity, inner_msd, core_msd = refs[:3]
+            refs = refs[3:]
         state, outs = refs[: state_size(index)], refs[state_size(index) :]
         for row in range(ROWS):
             raw = partial[row] + column_product(halo, blocks, row, 3)
-            term, summed, msd = advance(index, coeffs, parity, counts, state, (3,), 0, row, raw)
+            term, summed, msd = advance(index, coeffs, mask, state, (3,), 0, row, raw)
             if not last:
                 message = outs[row]
                 message[0] = core[row, 0]
@@ -209,7 +219,8 @@
                 message[2] = inner[row, 1]
                 message[3] = term.astype(jnp.bfloat16)
                 outs[2][row, 0] = summed
-                outs[3][row, 0] = term
+                if index < TERMS - 2:
+                    outs[3][row, 0] = term
                 continue
             displacements, msd_out = outs
             pieces = [core[row, 0], inner[row, 0], inner[row, 1], summed.astype(jnp.bfloat16)]
@@ -252,11 +263,11 @@
             pairs = [(i, i ^ 1) for i in range(size)]
         return lax.ppermute(value, axis, pairs)
 
-    far, near = pl.pallas_call(
+    far, near, mask = pl.pallas_call(
         start_kernel,
-        out_shape=(rounded, rounded),
+        out_shape=(rounded, rounded, jax.ShapeDtypeStruct((ROWS, COLS, 1, dofs), jnp.float32)),
         in_specs=[smem, smem, vmem],
-        out_specs=(vmem, vmem),
+        out_specs=(vmem, vmem, vmem),
         compiler_params=params,
         name="start",
     )(parity, counts, probes)
@@ -269,7 +280,7 @@
         return pl.pallas_call(
             body,
             out_shape=outs,
-            in_specs=[smem, smem] + [vmem] * (len(operands) - 2),
+            in_specs=[smem if operand is parity else vmem for operand in operands],
             out_specs=tuple([vmem] * len(outs)),
             compiler_params=params,
             cost_estimate=cost(pairs),
@@ -318,20 +329,20 @@
         def state(name, index=index, last=last):
             return saved[name] + (start if index <= 2 or last else [])
 
-        def outputs(cols, last=last):
+        def outputs(cols, index=index, last=last):
             if last:
                 mean = jax.ShapeDtypeStruct((ROWS, cols, 1, dofs), jnp.float32)
                 return (column_state(cols, jnp.bfloat16), mean)
             wide = column_state(cols, jnp.float32)
-            return (column_state(cols, jnp.bfloat16), wide, wide)
-
-        def keep(name, summed, term, index=index):
+            return (column_state(cols, jnp.bfloat16),) + (wide,) * (2 if index < TERMS - 2 else 1)
+
+        def keep(name, summed, term=None, index=index):
             terms[name].append(term)
             saved[name] = [summed] + ([terms[name][-2]] if index >= 2 else [])
 
         if index == 1:
             terms = {"inner": [], "core": [], "chip": []}
-        fixed = [parity, counts]
+        fixed = [mask]
         core_raw, chip_raw, inner, *rest = run(
             make_rows(index, coeffs),
             fixed + [halo_far, halo_near, held, partial] + state("inner"),
@@ -346,14 +357,14 @@
         )
         operands = fixed + [halo_chip, held, chip_raw, inner, core]
         if last:
-            operands += [rest[0], core_rest[0]]
+            operands += [parity, rest[0], core_rest[0]]
             outs = (
                 jax.ShapeDtypeStruct(probes.shape, jnp.bfloat16),
                 jax.ShapeDtypeStruct((ROWS, COLS, dofs), jnp.float32),
             )
         else:
             wide = column_state(1, jnp.float32)
-            outs = (rounded, rounded, wide, wide)
+            outs = (rounded, rounded) + (wide,) * (2 if index < TERMS - 2 else 1)
         results = run(make_chip(index, coeffs), operands + state("chip"), outs, 6)
         if not last:
             far, near = results[:2]

time: 164 us -> 159 us (0.970); the launches traced: 161 us -> 159 us
  waiting for transfers between devices: 56.8 us -> 74.9 us
  Pallas kernels: 65.3 us -> 52 us
  starting transfers between devices: 36.1 us -> 28.8 us
    ppermute x28, waiting for transfers between devices: 56.8 us -> 74.9 us  [swap(): return lax.ppermute(value, axis, pairs)]
    pallas_call x22, Pallas kernels: 36.5 us -> 23.3 us  [the longest x21 22.6 us: run(): pl.pallas_call(body, out_shape=outs, in_specs=[smem if operand is parity...]
    ppermute x28, starting transfers between devices: 36.1 us -> 28.8 us  [swap(): return lax.ppermute(value, axis, pairs)]
  transfers between devices with their start and end apart: 28 -> 28, of which waited for: 18 -> 18; matrix products, arithmetic and copies ran while one was open for 0% -> 0% of each run, Pallas kernels for 34% -> 28%
where the time goes in v1:
time: 159 us
  waiting for transfers between devices  74.9 us (47%)
  Pallas kernels  52 us (33%)
  starting transfers between devices  28.8 us (18%)
  local copies, waits for them, and re-layouts  1.68 us (1%)
    ppermute x28, waiting for transfers between devices, swap(): return lax.ppermute(value, axis, pairs)  74.9 us
    ppermute x28, starting transfers between devices, swap(): return lax.ppermute(value, axis, pairs)  28.8 us
    pallas_call x21, Pallas kernels, run(): pl.pallas_call(body, out_shape=outs, in_specs=[smem if operand is parity...  22.6 us
    pallas_call x6, Pallas kernels, local(): pl.pallas_call(own_kernel, out_shape=raw, in_specs=[vmem, vmem, vmem], ou...  19.1 us
    pallas_call x1, Pallas kernels, local(): pl.pallas_call(load_kernel, out_shape=(pltpu.VMEM(blocks.shape, blocks.dt...  9.48 us
  transfers between devices with their start and end apart: 28, of which 18 were waited for; matrix products, arithmetic and copies ran while one was open for 0% of the time, Pallas kernels for 28%

profile of v1, /device:TPU:97, one launch (start us, length us, event | category | flops | bytes accessed | tf_op | source)
XLA Modules:
  0.0 158.5 jit_solution(6566909332844662031)
XLA Ops:
  3.0 5.2 %collective-permute-start = (bf16[4,64,384]{2,1,0:T(8,128)(2,1)S(1)}, bf16[4,64,384]{2,1,0:T(8,128)(2,1)S(1)}, u32[]{:S(2)}, u32[]{:S(2)}) collective-permute-start(bf16[4,64,384]{2,1,0:T(8,128)(2,1)S(1)} %get-tuple-element.118.far.refs_0_.refs_1_.refs_2_.refs_5_), channel_id=1, source_target_pairs={{0,112},{16,32},{32,16},{48,64},{64,48},{80,96},{96,80},{112,0},{1... | collective-permute-start | bytes 589832 | tf_op jit(solution)/shard_map/ppermute | solution.py:264
  8.2 9.5 %load.1 = (bf16[2,4,9,384,384]{4,3,2,1,0:T(8,128)(2,1)S(1)}, f32[2,4,384,64]{3,2,1,0:T(8,128)S(1)}) custom-call(s32[2]{0:T(128)S(1)} %pad_add_fusion.parity.refs_0_, bf16[2,4,9,384,384]{4,3,2,1,0:T(8,128)(2,1)} %blocks.1, bf16[4,64,384]{2,1,0:T(8,128)(2,1)S(1)} %get-tuple-element.118.far.refs_0_.refs_1_.refs_2_.refs_5_, ...), custom_call_target="tpu_custom_call" | custom-call | bytes 42467328 | tf_op jit(solution)/shard_map/load/pallas_call | solution.py:297
  21.2 4.8 %collective-permute-done.2.halo = bf16[4,64,384]{2,1,0:T(8,128)(2,1)S(1)} collective-permute-done((bf16[4,64,384]{2,1,0:T(8,128)(2,1)S(1)}, bf16[4,64,384]{2,1,0:T(8,128)(2,1)S(1)}, u32[]{:S(2)}, u32[]{:S(2)}) %collective-permute-start.2) | collective-permute-done | bytes 196640 | tf_op jit(solution)/shard_map/ppermute | solution.py:264
  26.7 3.6 %collective-permute-start.4 = (bf16[4,64,384]{2,1,0:T(8,128)(2,1)S(1)}, bf16[4,64,384]{2,1,0:T(8,128)(2,1)S(1)}, u32[]{:S(2)}, u32[]{:S(2)}) collective-permute-start(bf16[4,64,384]{2,1,0:T(8,128)(2,1)S(1)} %get-tuple-element.131.far), channel_id=1, source_target_pairs={{0,112},{16,32},{32,16},{48,64},{64,48},{80,96},{96,80},{112,0},{1... | collective-permute-start | bytes 589832 | tf_op jit(solution)/shard_map/ppermute | solution.py:264
  30.3 3.2 %own.6.partial = f32[2,4,384,64]{3,2,1,0:T(8,128)S(1)} custom-call(bf16[4,64,384]{2,1,0:T(8,128)(2,1)S(1)} %get-tuple-element.131.far, bf16[4,64,384]{2,1,0:T(8,128)(2,1)S(1)} %get-tuple-element.132.near, bf16[2,4,9,384,384]{4,3,2,1,0:T(8,128)(2,1)S(1)} %get-tuple-element.124.blocks), custom_call_target="tpu_custom_call" | custom-call | flops 3019898880 | bytes 11796480 | tf_op jit(solution)/shard_map/own/pallas_call | solution.py:308
  35.6 4.3 %collective-permute-done.5.halo_near = bf16[4,64,384]{2,1,0:T(8,128)(2,1)S(1)} collective-permute-done((bf16[4,64,384]{2,1,0:T(8,128)(2,1)S(1)}, bf16[4,64,384]{2,1,0:T(8,128)(2,1)S(1)}, u32[]{:S(2)}, u32[]{:S(2)}) %collective-permute-start.5) | collective-permute-done | bytes 196640 | tf_op jit(solution)/shard_map/ppermute | solution.py:264
  42.8 4.8 %collective-permute-done.6.halo = bf16[4,64,384]{2,1,0:T(8,128)(2,1)S(1)} collective-permute-done((bf16[4,64,384]{2,1,0:T(8,128)(2,1)S(1)}, bf16[4,64,384]{2,1,0:T(8,128)(2,1)S(1)}, u32[]{:S(2)}, u32[]{:S(2)}) %collective-permute-start.6) | collective-permute-done | bytes 196640 | tf_op jit(solution)/shard_map/ppermute | solution.py:264
  51.4 3.2 %own.7.partial = f32[2,4,384,64]{3,2,1,0:T(8,128)S(1)} custom-call(bf16[4,64,384]{2,1,0:T(8,128)(2,1)S(1)} %get-tuple-element.145.far, bf16[4,64,384]{2,1,0:T(8,128)(2,1)S(1)} %get-tuple-element.146.near, bf16[2,4,9,384,384]{4,3,2,1,0:T(8,128)(2,1)S(1)} %get-tuple-element.124.blocks), custom_call_target="tpu_custom_call" | custom-call | flops 3019898880 | bytes 11796480 | tf_op jit(solution)/shard_map/own/pallas_call | solution.py:308
  57.2 4.3 %collective-permute-done.9.halo_near = bf16[4,64,384]{2,1,0:T(8,128)(2,1)S(1)} collective-permute-done((bf16[4,64,384]{2,1,0:T(8,128)(2,1)S(1)}, bf16[4,64,384]{2,1,0:T(8,128)(2,1)S(1)}, u32[]{:S(2)}, u32[]{:S(2)}) %collective-permute-start.9) | collective-permute-done | bytes 196640 | tf_op jit(solution)/shard_map/ppermute | solution.py:264
  64.4 4.8 %collective-permute-done.10.halo = bf16[4,64,384]{2,1,0:T(8,128)(2,1)S(1)} collective-permute-done((bf16[4,64,384]{2,1,0:T(8,128)(2,1)S(1)}, bf16[4,64,384]{2,1,0:T(8,128)(2,1)S(1)}, u32[]{:S(2)}, u32[]{:S(2)}) %collective-permute-start.10) | collective-permute-done | bytes 196640 | tf_op jit(solution)/shard_map/ppermute | solution.py:264
  69.9 6.0 %collective-permute-start.12 = (bf16[4,64,384]{2,1,0:T(8,128)(2,1)S(1)}, bf16[4,64,384]{2,1,0:T(8,128)(2,1)S(1)}, u32[]{:S(2)}, u32[]{:S(2)}) collective-permute-start(bf16[4,64,384]{2,1,0:T(8,128)(2,1)S(1)} %get-tuple-element.162.far), channel_id=1, source_target_pairs={{0,112},{16,32},{32,16},{48,64},{64,48},{80,96},{96,80},{112,0},{1... | collective-permute-start | bytes 589832 | tf_op jit(solution)/shard_map/ppermute | solution.py:264
  75.9 3.2 %own.8.partial = f32[2,4,384,64]{3,2,1,0:T(8,128)S(1)} custom-call(bf16[4,64,384]{2,1,0:T(8,128)(2,1)S(1)} %get-tuple-element.162.far, bf16[4,64,384]{2,1,0:T(8,128)(2,1)S(1)} %get-tuple-element.163.near, bf16[2,4,9,384,384]{4,3,2,1,0:T(8,128)(2,1)S(1)} %get-tuple-element.124.blocks), custom_call_target="tpu_custom_call" | custom-call | flops 3019898880 | bytes 11796480 | tf_op jit(solution)/shard_map/own/pallas_call | solution.py:308
  79.1 3.8 %collective-permute-done.13.halo_near = bf16[4,64,384]{2,1,0:T(8,128)(2,1)S(1)} collective-permute-done((bf16[4,64,384]{2,1,0:T(8,128)(2,1)S(1)}, bf16[4,64,384]{2,1,0:T(8,128)(2,1)S(1)}, u32[]{:S(2)}, u32[]{:S(2)}) %collective-permute-start.13) | collective-permute-done | bytes 196640 | tf_op jit(solution)/shard_map/ppermute | solution.py:264
  85.5 4.8 %collective-permute-done.14.halo = bf16[4,64,384]{2,1,0:T(8,128)(2,1)S(1)} collective-permute-done((bf16[4,64,384]{2,1,0:T(8,128)(2,1)S(1)}, bf16[4,64,384]{2,1,0:T(8,128)(2,1)S(1)}, u32[]{:S(2)}, u32[]{:S(2)}) %collective-permute-start.14) | collective-permute-done | bytes 196640 | tf_op jit(solution)/shard_map/ppermute | solution.py:264
  91.0 5.8 %collective-permute-start.16 = (bf16[4,64,384]{2,1,0:T(8,128)(2,1)S(1)}, bf16[4,64,384]{2,1,0:T(8,128)(2,1)S(1)}, u32[]{:S(2)}, u32[]{:S(2)}) collective-permute-start(bf16[4,64,384]{2,1,0:T(8,128)(2,1)S(1)} %get-tuple-element.179.far), channel_id=1, source_target_pairs={{0,112},{16,32},{32,16},{48,64},{64,48},{80,96},{96,80},{112,0},{1... | collective-permute-start | bytes 589832 | tf_op jit(solution)/shard_map/ppermute | solution.py:264
  96.8 3.2 %own.9.partial = f32[2,4,384,64]{3,2,1,0:T(8,128)S(1)} custom-call(bf16[4,64,384]{2,1,0:T(8,128)(2,1)S(1)} %get-tuple-element.179.far, bf16[4,64,384]{2,1,0:T(8,128)(2,1)S(1)} %get-tuple-element.180.near, bf16[2,4,9,384,384]{4,3,2,1,0:T(8,128)(2,1)S(1)} %get-tuple-element.124.blocks), custom_call_target="tpu_custom_call" | custom-call | flops 3019898880 | bytes 11796480 | tf_op jit(solution)/shard_map/own/pallas_call | solution.py:308
  100.2 4.1 %collective-permute-done.17.halo_near = bf16[4,64,384]{2,1,0:T(8,128)(2,1)S(1)} collective-permute-done((bf16[4,64,384]{2,1,0:T(8,128)(2,1)S(1)}, bf16[4,64,384]{2,1,0:T(8,128)(2,1)S(1)}, u32[]{:S(2)}, u32[]{:S(2)}) %collective-permute-start.17) | collective-permute-done | bytes 196640 | tf_op jit(solution)/shard_map/ppermute | solution.py:264
  107.1 9.4 %collective-permute-done.18.halo = bf16[4,64,384]{2,1,0:T(8,128)(2,1)S(1)} collective-permute-done((bf16[4,64,384]{2,1,0:T(8,128)(2,1)S(1)}, bf16[4,64,384]{2,1,0:T(8,128)(2,1)S(1)}, u32[]{:S(2)}, u32[]{:S(2)}) %collective-permute-start.18) | collective-permute-done | bytes 196640 | tf_op jit(solution)/shard_map/ppermute | solution.py:264
  119.1 3.2 %own.10.partial = f32[2,4,384,64]{3,2,1,0:T(8,128)S(1)} custom-call(bf16[4,64,384]{2,1,0:T(8,128)(2,1)S(1)} %get-tuple-element.196.far, bf16[4,64,384]{2,1,0:T(8,128)(2,1)S(1)} %get-tuple-element.197.near, bf16[2,4,9,384,384]{4,3,2,1,0:T(8,128)(2,1)S(1)} %get-tuple-element.124.blocks), custom_call_target="tpu_custom_call" | custom-call | flops 3019898880 | bytes 11796480 | tf_op jit(solution)/shard_map/own/pallas_call | solution.py:308
  122.3 3.3 %collective-permute-done.20.halo_far = bf16[4,64,384]{2,1,0:T(8,128)(2,1)S(1)} collective-permute-done((bf16[4,64,384]{2,1,0:T(8,128)(2,1)S(1)}, bf16[4,64,384]{2,1,0:T(8,128)(2,1)S(1)}, u32[]{:S(2)}, u32[]{:S(2)}) %collective-permute-start.20) | collective-permute-done | bytes 196640 | tf_op jit(solution)/shard_map/ppermute | solution.py:264
  129.8 6.9 %collective-permute-done.22.halo = bf16[4,64,384]{2,1,0:T(8,128)(2,1)S(1)} collective-permute-done((bf16[4,64,384]{2,1,0:T(8,128)(2,1)S(1)}, bf16[4,64,384]{2,1,0:T(8,128)(2,1)S(1)}, u32[]{:S(2)}, u32[]{:S(2)}) %collective-permute-start.22) | collective-permute-done | bytes 196640 | tf_op jit(solution)/shard_map/ppermute | solution.py:264
  137.6 3.2 %own.11.partial = f32[2,4,384,64]{3,2,1,0:T(8,128)S(1)} custom-call(bf16[4,64,384]{2,1,0:T(8,128)(2,1)S(1)} %get-tuple-element.213.far, bf16[4,64,384]{2,1,0:T(8,128)(2,1)S(1)} %get-tuple-element.214.near, bf16[2,4,9,384,384]{4,3,2,1,0:T(8,128)(2,1)S(1)} %get-tuple-element.124.blocks), custom_call_target="tpu_custom_call" | custom-call | flops 3019898880 | bytes 11796480 | tf_op jit(solution)/shard_map/own/pallas_call | solution.py:308
  140.8 4.9 %collective-permute-done.24.halo_far = bf16[4,64,384]{2,1,0:T(8,128)(2,1)S(1)} collective-permute-done((bf16[4,64,384]{2,1,0:T(8,128)(2,1)S(1)}, bf16[4,64,384]{2,1,0:T(8,128)(2,1)S(1)}, u32[]{:S(2)}, u32[]{:S(2)}) %collective-permute-start.24) | collective-permute-done | bytes 196640 | tf_op jit(solution)/shard_map/ppermute | solution.py:264
  151.8 4.8 %collective-permute-done.26.halo = bf16[4,64,384]{2,1,0:T(8,128)(2,1)S(1)} collective-permute-done((bf16[4,64,384]{2,1,0:T(8,128)(2,1)S(1)}, bf16[4,64,384]{2,1,0:T(8,128)(2,1)S(1)}, u32[]{:S(2)}, u32[]{:S(2)}) %collective-permute-start.26) | collective-permute-done | bytes 196640 | tf_op jit(solution)/shard_map/ppermute | solution.py:264
  (77 shorter events, 43.2 us)
Async XLA Ops:
  3.0 14.7 %collective-permute-start = (bf16[4,64,384]{2,1,0:T(8,128)(2,1)S(1)}, bf16[4,64,384]{2,1,0:T(8,128)(2,1)S(1)}, u32[]{:S(2)}, u32[]{:S(2)}) collective-permute-start(bf16[4,64,384]{2,1,0:T(8,128)(2,1)S(1)} %get-tuple-element.118.far.refs_0_.refs_1_.refs_2_.refs_5_), channel_id=1, source_target_pairs={{0,112},{16,32},{32,16},{48,64},{64,48},{80,96},{96,80},{112,0},{1... | collective-permute-start | bytes 589832 | tf_op jit(solution)/shard_map/ppermute | solution.py:264
  8.2 9.5 %collective-permute-start.1 = (bf16[4,64,384]{2,1,0:T(8,128)(2,1)S(1)}, bf16[4,64,384]{2,1,0:T(8,128)(2,1)S(1)}, u32[]{:S(2)}, u32[]{:S(2)}) collective-permute-start(bf16[4,64,384]{2,1,0:T(8,128)(2,1)S(1)} %get-tuple-element.119.near.refs_1_.refs_2_.refs_3_.refs_6_), channel_id=1, source_target_pairs={{0,16},{16,0},{32,48},{48,32},{64,80},{80,64},{96,112},{112,96},{1... | collective-permute-start | bytes 589832 | tf_op jit(solution)/shard_map/ppermute | solution.py:264
  17.8 2.7 %collective-permute-start.3 = (bf16[4,64,384]{2,1,0:T(8,128)(2,1)S(1)}, bf16[4,64,384]{2,1,0:T(8,128)(2,1)S(1)}, u32[]{:S(2)}, u32[]{:S(2)}) collective-permute-start(bf16[4,64,384]{2,1,0:T(8,128)(2,1)S(1)} %get-tuple-element.128), channel_id=1, source_target_pairs={{0,1},{1,0},{2,3},{3,2},{4,5},{5,4},{6,7},{7,6},{8,9},{9,8},{10,11... | collective-permute-start | bytes 589832 | tf_op jit(solution)/shard_map/ppermute | solution.py:264
  18.8 7.2 %collective-permute-start.2 = (bf16[4,64,384]{2,1,0:T(8,128)(2,1)S(1)}, bf16[4,64,384]{2,1,0:T(8,128)(2,1)S(1)}, u32[]{:S(2)}, u32[]{:S(2)}) collective-permute-start(bf16[4,64,384]{2,1,0:T(8,128)(2,1)S(1)} %get-tuple-element.123), channel_id=1, source_target_pairs={{0,15},{1,2},{2,1},{3,4},{4,3},{5,6},{6,5},{7,8},{8,7},{9,10},{10,... | collective-permute-start | bytes 589832 | tf_op jit(solution)/shard_map/ppermute | solution.py:264
  26.7 8.9 %collective-permute-start.4 = (bf16[4,64,384]{2,1,0:T(8,128)(2,1)S(1)}, bf16[4,64,384]{2,1,0:T(8,128)(2,1)S(1)}, u32[]{:S(2)}, u32[]{:S(2)}) collective-permute-start(bf16[4,64,384]{2,1,0:T(8,128)(2,1)S(1)} %get-tuple-element.131.far), channel_id=1, source_target_pairs={{0,112},{16,32},{32,16},{48,64},{64,48},{80,96},{96,80},{112,0},{1... | collective-permute-start | bytes 589832 | tf_op jit(solution)/shard_map/ppermute | solution.py:264
  30.3 9.6 %collective-permute-start.5 = (bf16[4,64,384]{2,1,0:T(8,128)(2,1)S(1)}, bf16[4,64,384]{2,1,0:T(8,128)(2,1)S(1)}, u32[]{:S(2)}, u32[]{:S(2)}) collective-permute-start(bf16[4,64,384]{2,1,0:T(8,128)(2,1)S(1)} %get-tuple-element.132.near), channel_id=1, source_target_pairs={{0,16},{16,0},{32,48},{48,32},{64,80},{80,64},{96,112},{112,96},{1... | collective-permute-start | bytes 589832 | tf_op jit(solution)/shard_map/ppermute | solution.py:264
  39.9 2.2 %collective-permute-start.7 = (bf16[4,64,384]{2,1,0:T(8,128)(2,1)S(1)}, bf16[4,64,384]{2,1,0:T(8,128)(2,1)S(1)}, u32[]{:S(2)}, u32[]{:S(2)}) collective-permute-start(bf16[4,64,384]{2,1,0:T(8,128)(2,1)S(1)} %get-tuple-element.140), channel_id=1, source_target_pairs={{0,1},{1,0},{2,3},{3,2},{4,5},{5,4},{6,7},{7,6},{8,9},{9,8},{10,11... | collective-permute-start | bytes 589832 | tf_op jit(solution)/shard_map/ppermute | solution.py:264
  40.4 7.2 %collective-permute-start.6 = (bf16[4,64,384]{2,1,0:T(8,128)(2,1)S(1)}, bf16[4,64,384]{2,1,0:T(8,128)(2,1)S(1)}, u32[]{:S(2)}, u32[]{:S(2)}) collective-permute-start(bf16[4,64,384]{2,1,0:T(8,128)(2,1)S(1)} %get-tuple-element.135), channel_id=1, source_target_pairs={{0,15},{1,2},{2,1},{3,4},{4,3},{5,6},{6,5},{7,8},{8,7},{9,10},{10,... | collective-permute-start | bytes 589832 | tf_op jit(solution)/shard_map/ppermute | solution.py:264
  48.3 8.9 %collective-permute-start.8 = (bf16[4,64,384]{2,1,0:T(8,128)(2,1)S(1)}, bf16[4,64,384]{2,1,0:T(8,128)(2,1)S(1)}, u32[]{:S(2)}, u32[]{:S(2)}) collective-permute-start(bf16[4,64,384]{2,1,0:T(8,128)(2,1)S(1)} %get-tuple-element.145.far), channel_id=1, source_target_pairs={{0,112},{16,32},{32,16},{48,64},{64,48},{80,96},{96,80},{112,0},{1... | collective-permute-start | bytes 589832 | tf_op jit(solution)/shard_map/ppermute | solution.py:264
  51.4 10.1 %collective-permute-start.9 = (bf16[4,64,384]{2,1,0:T(8,128)(2,1)S(1)}, bf16[4,64,384]{2,1,0:T(8,128)(2,1)S(1)}, u32[]{:S(2)}, u32[]{:S(2)}) collective-permute-start(bf16[4,64,384]{2,1,0:T(8,128)(2,1)S(1)} %get-tuple-element.146.near), channel_id=1, source_target_pairs={{0,16},{16,0},{32,48},{48,32},{64,80},{80,64},{96,112},{112,96},{1... | collective-permute-start | bytes 589832 | tf_op jit(solution)/shard_map/ppermute | solution.py:264
  62.0 7.2 %collective-permute-start.10 = (bf16[4,64,384]{2,1,0:T(8,128)(2,1)S(1)}, bf16[4,64,384]{2,1,0:T(8,128)(2,1)S(1)}, u32[]{:S(2)}, u32[]{:S(2)}) collective-permute-start(bf16[4,64,384]{2,1,0:T(8,128)(2,1)S(1)} %get-tuple-element.149), channel_id=1, source_target_pairs={{0,15},{1,2},{2,1},{3,4},{4,3},{5,6},{6,5},{7,8},{8,7},{9,10},{10,... | collective-permute-start | bytes 589832 | tf_op jit(solution)/shard_map/ppermute | solution.py:264
  69.9 9.2 %collective-permute-start.12 = (bf16[4,64,384]{2,1,0:T(8,128)(2,1)S(1)}, bf16[4,64,384]{2,1,0:T(8,128)(2,1)S(1)}, u32[]{:S(2)}, u32[]{:S(2)}) collective-permute-start(bf16[4,64,384]{2,1,0:T(8,128)(2,1)S(1)} %get-tuple-element.162.far), channel_id=1, source_target_pairs={{0,112},{16,32},{32,16},{48,64},{64,48},{80,96},{96,80},{112,0},{1... | collective-permute-start | bytes 589832 | tf_op jit(solution)/shard_map/ppermute | solution.py:264
  75.9 7.0 %collective-permute-start.13 = (bf16[4,64,384]{2,1,0:T(8,128)(2,1)S(1)}, bf16[4,64,384]{2,1,0:T(8,128)(2,1)S(1)}, u32[]{:S(2)}, u32[]{:S(2)}) collective-permute-start(bf16[4,64,384]{2,1,0:T(8,128)(2,1)S(1)} %get-tuple-element.163.near), channel_id=1, source_target_pairs={{0,16},{16,0},{32,48},{48,32},{64,80},{80,64},{96,112},{112,96},{1... | collective-permute-start | bytes 589832 | tf_op jit(solution)/shard_map/ppermute | solution.py:264
  83.0 7.3 %collective-permute-start.14 = (bf16[4,64,384]{2,1,0:T(8,128)(2,1)S(1)}, bf16[4,64,384]{2,1,0:T(8,128)(2,1)S(1)}, u32[]{:S(2)}, u32[]{:S(2)}) collective-permute-start(bf16[4,64,384]{2,1,0:T(8,128)(2,1)S(1)} %get-tuple-element.166), channel_id=1, source_target_pairs={{0,15},{1,2},{2,1},{3,4},{4,3},{5,6},{6,5},{7,8},{8,7},{9,10},{10,... | collective-permute-start | bytes 589832 | tf_op jit(solution)/shard_map/ppermute | solution.py:264
  91.0 9.2 %collective-permute-start.16 = (bf16[4,64,384]{2,1,0:T(8,128)(2,1)S(1)}, bf16[4,64,384]{2,1,0:T(8,128)(2,1)S(1)}, u32[]{:S(2)}, u32[]{:S(2)}) collective-permute-start(bf16[4,64,384]{2,1,0:T(8,128)(2,1)S(1)} %get-tuple-element.179.far), channel_id=1, source_target_pairs={{0,112},{16,32},{32,16},{48,64},{64,48},{80,96},{96,80},{112,0},{1... | collective-permute-start | bytes 589832 | tf_op jit(solution)/shard_map/ppermute | solution.py:264
  96.8 7.5 %collective-permute-start.17 = (bf16[4,64,384]{2,1,0:T(8,128)(2,1)S(1)}, bf16[4,64,384]{2,1,0:T(8,128)(2,1)S(1)}, u32[]{:S(2)}, u32[]{:S(2)}) collective-permute-start(bf16[4,64,384]{2,1,0:T(8,128)(2,1)S(1)} %get-tuple-element.180.near), channel_id=1, source_target_pairs={{0,16},{16,0},{32,48},{48,32},{64,80},{80,64},{96,112},{112,96},{1... | collective-permute-start | bytes 589832 | tf_op jit(solution)/shard_map/ppermute | solution.py:264
  104.5 12.1 %collective-permute-start.18 = (bf16[4,64,384]{2,1,0:T(8,128)(2,1)S(1)}, bf16[4,64,384]{2,1,0:T(8,128)(2,1)S(1)}, u32[]{:S(2)}, u32[]{:S(2)}) collective-permute-start(bf16[4,64,384]{2,1,0:T(8,128)(2,1)S(1)} %get-tuple-element.183), channel_id=1, source_target_pairs={{0,15},{1,2},{2,1},{3,4},{4,3},{5,6},{6,5},{7,8},{8,7},{9,10},{10,... | collective-permute-start | bytes 589832 | tf_op jit(solution)/shard_map/ppermute | solution.py:264
  117.3 8.3 %collective-permute-start.20 = (bf16[4,64,384]{2,1,0:T(8,128)(2,1)S(1)}, bf16[4,64,384]{2,1,0:T(8,128)(2,1)S(1)}, u32[]{:S(2)}, u32[]{:S(2)}) collective-permute-start(bf16[4,64,384]{2,1,0:T(8,128)(2,1)S(1)} %get-tuple-element.196.far), channel_id=1, source_target_pairs={{0,112},{16,32},{32,16},{48,64},{64,48},{80,96},{96,80},{112,0},{1... | collective-permute-start | bytes 589832 | tf_op jit(solution)/shard_map/ppermute | solution.py:264
  119.1 8.1 %collective-permute-start.21 = (bf16[4,64,384]{2,1,0:T(8,128)(2,1)S(1)}, bf16[4,64,384]{2,1,0:T(8,128)(2,1)S(1)}, u32[]{:S(2)}, u32[]{:S(2)}) collective-permute-start(bf16[4,64,384]{2,1,0:T(8,128)(2,1)S(1)} %get-tuple-element.197.near), channel_id=1, source_target_pairs={{0,16},{16,0},{32,48},{48,32},{64,80},{80,64},{96,112},{112,96},{1... | collective-permute-start | bytes 589832 | tf_op jit(solution)/shard_map/ppermute | solution.py:264
  127.4 9.4 %collective-permute-start.22 = (bf16[4,64,384]{2,1,0:T(8,128)(2,1)S(1)}, bf16[4,64,384]{2,1,0:T(8,128)(2,1)S(1)}, u32[]{:S(2)}, u32[]{:S(2)}) collective-permute-start(bf16[4,64,384]{2,1,0:T(8,128)(2,1)S(1)} %get-tuple-element.200), channel_id=1, source_target_pairs={{0,15},{1,2},{2,1},{3,4},{4,3},{5,6},{6,5},{7,8},{8,7},{9,10},{10,... | collective-permute-start | bytes 589832 | tf_op jit(solution)/shard_map/ppermute | solution.py:264
  137.4 8.3 %collective-permute-start.24 = (bf16[4,64,384]{2,1,0:T(8,128)(2,1)S(1)}, bf16[4,64,384]{2,1,0:T(8,128)(2,1)S(1)}, u32[]{:S(2)}, u32[]{:S(2)}) collective-permute-start(bf16[4,64,384]{2,1,0:T(8,128)(2,1)S(1)} %get-tuple-element.213.far), channel_id=1, source_target_pairs={{0,112},{16,32},{32,16},{48,64},{64,48},{80,96},{96,80},{112,0},{1... | collective-permute-start | bytes 589832 | tf_op jit(solution)/shard_map/ppermute | solution.py:264
  137.5 11.3 %collective-permute-start.25 = (bf16[4,64,384]{2,1,0:T(8,128)(2,1)S(1)}, bf16[4,64,384]{2,1,0:T(8,128)(2,1)S(1)}, u32[]{:S(2)}, u32[]{:S(2)}) collective-permute-start(bf16[4,64,384]{2,1,0:T(8,128)(2,1)S(1)} %get-tuple-element.214.near), channel_id=1, source_target_pairs={{0,16},{16,0},{32,48},{48,32},{64,80},{80,64},{96,112},{112,96},{1... | collective-permute-start | bytes 589832 | tf_op jit(solution)/shard_map/ppermute | solution.py:264
  148.9 2.2 %collective-permute-start.27 = (bf16[4,64,384]{2,1,0:T(8,128)(2,1)S(1)}, bf16[4,64,384]{2,1,0:T(8,128)(2,1)S(1)}, u32[]{:S(2)}, u32[]{:S(2)}) collective-permute-start(bf16[4,64,384]{2,1,0:T(8,128)(2,1)S(1)} %get-tuple-element.223), channel_id=1, source_target_pairs={{0,1},{1,0},{2,3},{3,2},{4,5},{5,4},{6,7},{7,6},{8,9},{9,8},{10,11... | collective-permute-start | bytes 589832 | tf_op jit(solution)/shard_map/ppermute | solution.py:264
  149.3 7.2 %collective-permute-start.26 = (bf16[4,64,384]{2,1,0:T(8,128)(2,1)S(1)}, bf16[4,64,384]{2,1,0:T(8,128)(2,1)S(1)}, u32[]{:S(2)}, u32[]{:S(2)}) collective-permute-start(bf16[4,64,384]{2,1,0:T(8,128)(2,1)S(1)} %get-tuple-element.217), channel_id=1, source_target_pairs={{0,15},{1,2},{2,1},{3,4},{4,3},{5,6},{6,5},{7,8},{8,7},{9,10},{10,... | collective-permute-start | bytes 589832 | tf_op jit(solution)/shard_map/ppermute | solution.py:264
  (8 other events, 30.5 us)

commit v2 on v1

--- a/solution.py
+++ b/solution.py
@@ -116,6 +116,12 @@
             total[row, col] = own_product(far, near, blocks, row, col)
 
 
+def near_kernel(halo_near, blocks, partial, total):
+    for col in range(COLS):
+        total[1, col] = partial[1, col] + row_product(halo_near, blocks, 1, col)
+    total[0] = partial[0]
+
+
 def row_product(ref, blocks, row, col):
     pieces = []
     for step_col in range(3):
@@ -161,11 +167,13 @@
 
 
 def make_rows(index, coeffs):
-    def rows(mask, halo_far, halo_near, blocks, partial, *refs):
+    def rows(mask, halo_far, blocks, partial, *refs):
         state, outs = refs[: state_size(index)], refs[state_size(index) :]
-        for row, ref in enumerate((halo_far, halo_near)):
+        for row in range(ROWS):
             for col in (1, 2, 0, 3):
-                raw = partial[row, col] + row_product(ref, blocks, row, col)
+                raw = partial[row, col]
+                if row == 0:
+                    raw = raw + row_product(halo_far, blocks, row, col)
                 if col in (0, 3):
                     outs[0 if col == 0 else 1][row] = raw
                     continue
@@ -314,7 +322,18 @@
                 cost_estimate=cost(40),
                 name="own",
             )(far, near, held)
-        halo_far, halo_near, partial = lax.optimization_barrier((halo_far, halo_near, partial))
+        halo_near, partial = lax.optimization_barrier((halo_near, partial))
+        partial = pl.pallas_call(
+            near_kernel,
+            out_shape=raw,
+            in_specs=[vmem] * 3,
+            out_specs=vmem,
+            input_output_aliases={2: 0},
+            compiler_params=params,
+            cost_estimate=cost(10),
+            name="near",
+        )(halo_near, held, partial)
+        halo_far, partial = lax.optimization_barrier((halo_far, partial))
         core_edge, chip_edge = pl.pallas_call(
             edge_kernel,
             out_shape=(rounded, rounded),
@@ -345,7 +364,7 @@
         fixed = [mask]
         core_raw, chip_raw, inner, *rest = run(
             make_rows(index, coeffs),
-            fixed + [halo_far, halo_near, held, partial] + state("inner"),
+            fixed + [halo_far, held, partial] + state("inner"),
             (edge, edge) + outputs(2),
             20,
         )

time: 159 us -> 169 us (1.063)
  the two profiles are of different devices: /device:TPU:97 before, /device:TPU:0 now
where the time goes in v2:
time: 169 us
  waiting for transfers between devices  61.2 us (36%)
  Pallas kernels  53.9 us (32%)
  starting transfers between devices  51 us (30%)
    ppermute x28, waiting for transfers between devices, swap(): return lax.ppermute(value, axis, pairs)  61.2 us
    ppermute x28, starting transfers between devices, swap(): return lax.ppermute(value, axis, pairs)  51 us
    pallas_call x6, Pallas kernels, local(): pl.pallas_call(own_kernel, out_shape=raw, in_specs=[vmem, vmem, vmem], ou...  19.1 us
    pallas_call x21, Pallas kernels, run(): pl.pallas_call(body, out_shape=outs, in_specs=[smem if operand is parity...  17.4 us
    pallas_call x1, Pallas kernels, local(): pl.pallas_call(load_kernel, out_shape=(pltpu.VMEM(blocks.shape, blocks.dt...  9.48 us
    pallas_call x7, Pallas kernels, local(): pl.pallas_call(near_kernel, out_shape=raw, in_specs=[vmem] * 3, out_specs...  7.04 us
  transfers between devices with their start and end apart: 28, of which 13 were waited for; matrix products, arithmetic and copies ran while one was open for 0% of the time, Pallas kernels for 28%

profile of v2, /device:TPU:0, one launch (start us, length us, event | category | flops | bytes accessed | tf_op | source)
XLA Modules:
  0.0 169.0 jit_solution(17684645356554836437)
XLA Ops:
  3.0 3.4 %collective-permute-start.1 = (bf16[4,64,384]{2,1,0:T(8,128)(2,1)S(1)}, bf16[4,64,384]{2,1,0:T(8,128)(2,1)S(1)}, u32[]{:S(2)}, u32[]{:S(2)}) collective-permute-start(bf16[4,64,384]{2,1,0:T(8,128)(2,1)S(1)} %get-tuple-element.126.near.refs_1_.refs_2_.refs_3_.refs_6_), channel_id=1, source_target_pairs={{0,16},{16,0},{32,48},{48,32},{64,80},{80,64},{96,112},{112,96},{1... | collective-permute-start | bytes 589832 | tf_op jit(solution)/shard_map/ppermute | solution.py:272
  9.0 9.5 %load.1 = (bf16[2,4,9,384,384]{4,3,2,1,0:T(8,128)(2,1)S(1)}, f32[2,4,384,64]{3,2,1,0:T(8,128)S(1)}) custom-call(s32[2]{0:T(128)S(1)} %pad_add_fusion.parity.refs_0_, bf16[2,4,9,384,384]{4,3,2,1,0:T(8,128)(2,1)} %blocks.1, bf16[4,64,384]{2,1,0:T(8,128)(2,1)S(1)} %get-tuple-element.125.far.refs_0_.refs_1_.refs_2_.refs_5_, ...), custom_call_target="tpu_custom_call" | custom-call | bytes 42467328 | tf_op jit(solution)/shard_map/load/pallas_call | solution.py:305
  19.6 5.2 %collective-permute-start.2 = (bf16[4,64,384]{2,1,0:T(8,128)(2,1)S(1)}, bf16[4,64,384]{2,1,0:T(8,128)(2,1)S(1)}, u32[]{:S(2)}, u32[]{:S(2)}) collective-permute-start(bf16[4,64,384]{2,1,0:T(8,128)(2,1)S(1)} %get-tuple-element.132), channel_id=1, source_target_pairs={{0,15},{1,2},{2,1},{3,4},{4,3},{5,6},{6,5},{7,8},{8,7},{9,10},{10,... | collective-permute-start | bytes 589832 | tf_op jit(solution)/shard_map/ppermute | solution.py:272
  31.7 3.2 %own.6.partial = f32[2,4,384,64]{3,2,1,0:T(8,128)S(1)} custom-call(bf16[4,64,384]{2,1,0:T(8,128)(2,1)S(1)} %get-tuple-element.139.far, bf16[4,64,384]{2,1,0:T(8,128)(2,1)S(1)} %get-tuple-element.140.near, bf16[2,4,9,384,384]{4,3,2,1,0:T(8,128)(2,1)S(1)} %get-tuple-element.129.blocks), custom_call_target="tpu_custom_call" | custom-call | flops 3019898880 | bytes 11796480 | tf_op jit(solution)/shard_map/own/pallas_call | solution.py:316
  34.9 5.7 %collective-permute-done.5.halo_near = bf16[4,64,384]{2,1,0:T(8,128)(2,1)S(1)} collective-permute-done((bf16[4,64,384]{2,1,0:T(8,128)(2,1)S(1)}, bf16[4,64,384]{2,1,0:T(8,128)(2,1)S(1)}, u32[]{:S(2)}, u32[]{:S(2)}) %collective-permute-start.5) | collective-permute-done | bytes 196640 | tf_op jit(solution)/shard_map/ppermute | solution.py:272
  41.8 5.6 %collective-permute-start.6 = (bf16[4,64,384]{2,1,0:T(8,128)(2,1)S(1)}, bf16[4,64,384]{2,1,0:T(8,128)(2,1)S(1)}, u32[]{:S(2)}, u32[]{:S(2)}) collective-permute-start(bf16[4,64,384]{2,1,0:T(8,128)(2,1)S(1)} %get-tuple-element.144), channel_id=1, source_target_pairs={{0,15},{1,2},{2,1},{3,4},{4,3},{5,6},{6,5},{7,8},{8,7},{9,10},{10,... | collective-permute-start | bytes 589832 | tf_op jit(solution)/shard_map/ppermute | solution.py:272
  49.0 4.3 %collective-permute-done.6.halo = bf16[4,64,384]{2,1,0:T(8,128)(2,1)S(1)} collective-permute-done((bf16[4,64,384]{2,1,0:T(8,128)(2,1)S(1)}, bf16[4,64,384]{2,1,0:T(8,128)(2,1)S(1)}, u32[]{:S(2)}, u32[]{:S(2)}) %collective-permute-start.6) | collective-permute-done | bytes 196640 | tf_op jit(solution)/shard_map/ppermute | solution.py:272
  54.3 3.2 %own.7.partial = f32[2,4,384,64]{3,2,1,0:T(8,128)S(1)} custom-call(bf16[4,64,384]{2,1,0:T(8,128)(2,1)S(1)} %get-tuple-element.154.far, bf16[4,64,384]{2,1,0:T(8,128)(2,1)S(1)} %get-tuple-element.155.near, bf16[2,4,9,384,384]{4,3,2,1,0:T(8,128)(2,1)S(1)} %get-tuple-element.129.blocks), custom_call_target="tpu_custom_call" | custom-call | flops 3019898880 | bytes 11796480 | tf_op jit(solution)/shard_map/own/pallas_call | solution.py:316
  57.5 6.1 %collective-permute-done.9.halo_near = bf16[4,64,384]{2,1,0:T(8,128)(2,1)S(1)} collective-permute-done((bf16[4,64,384]{2,1,0:T(8,128)(2,1)S(1)}, bf16[4,64,384]{2,1,0:T(8,128)(2,1)S(1)}, u32[]{:S(2)}, u32[]{:S(2)}) %collective-permute-start.9) | collective-permute-done | bytes 196640 | tf_op jit(solution)/shard_map/ppermute | solution.py:272
  64.8 5.1 %collective-permute-start.10 = (bf16[4,64,384]{2,1,0:T(8,128)(2,1)S(1)}, bf16[4,64,384]{2,1,0:T(8,128)(2,1)S(1)}, u32[]{:S(2)}, u32[]{:S(2)}) collective-permute-start(bf16[4,64,384]{2,1,0:T(8,128)(2,1)S(1)} %get-tuple-element.159), channel_id=1, source_target_pairs={{0,15},{1,2},{2,1},{3,4},{4,3},{5,6},{6,5},{7,8},{8,7},{9,10},{10,... | collective-permute-start | bytes 589832 | tf_op jit(solution)/shard_map/ppermute | solution.py:272
  71.5 4.0 %collective-permute-done.10.halo = bf16[4,64,384]{2,1,0:T(8,128)(2,1)S(1)} collective-permute-done((bf16[4,64,384]{2,1,0:T(8,128)(2,1)S(1)}, bf16[4,64,384]{2,1,0:T(8,128)(2,1)S(1)}, u32[]{:S(2)}, u32[]{:S(2)}) %collective-permute-start.10) | collective-permute-done | bytes 196640 | tf_op jit(solution)/shard_map/ppermute | solution.py:272
  76.5 3.2 %own.8.partial = f32[2,4,384,64]{3,2,1,0:T(8,128)S(1)} custom-call(bf16[4,64,384]{2,1,0:T(8,128)(2,1)S(1)} %get-tuple-element.172.far, bf16[4,64,384]{2,1,0:T(8,128)(2,1)S(1)} %get-tuple-element.173.near, bf16[2,4,9,384,384]{4,3,2,1,0:T(8,128)(2,1)S(1)} %get-tuple-element.129.blocks), custom_call_target="tpu_custom_call" | custom-call | flops 3019898880 | bytes 11796480 | tf_op jit(solution)/shard_map/own/pallas_call | solution.py:316
  79.7 6.1 %collective-permute-done.13.halo_near = bf16[4,64,384]{2,1,0:T(8,128)(2,1)S(1)} collective-permute-done((bf16[4,64,384]{2,1,0:T(8,128)(2,1)S(1)}, bf16[4,64,384]{2,1,0:T(8,128)(2,1)S(1)}, u32[]{:S(2)}, u32[]{:S(2)}) %collective-permute-start.13) | collective-permute-done | bytes 196640 | tf_op jit(solution)/shard_map/ppermute | solution.py:272
  86.9 5.5 %collective-permute-start.14 = (bf16[4,64,384]{2,1,0:T(8,128)(2,1)S(1)}, bf16[4,64,384]{2,1,0:T(8,128)(2,1)S(1)}, u32[]{:S(2)}, u32[]{:S(2)}) collective-permute-start(bf16[4,64,384]{2,1,0:T(8,128)(2,1)S(1)} %get-tuple-element.177), channel_id=1, source_target_pairs={{0,15},{1,2},{2,1},{3,4},{4,3},{5,6},{6,5},{7,8},{8,7},{9,10},{10,... | collective-permute-start | bytes 589832 | tf_op jit(solution)/shard_map/ppermute | solution.py:272
  94.1 4.8 %collective-permute-done.14.halo = bf16[4,64,384]{2,1,0:T(8,128)(2,1)S(1)} collective-permute-done((bf16[4,64,384]{2,1,0:T(8,128)(2,1)S(1)}, bf16[4,64,384]{2,1,0:T(8,128)(2,1)S(1)}, u32[]{:S(2)}, u32[]{:S(2)}) %collective-permute-start.14) | collective-permute-done | bytes 196640 | tf_op jit(solution)/shard_map/ppermute | solution.py:272
  100.0 3.2 %own.9.partial = f32[2,4,384,64]{3,2,1,0:T(8,128)S(1)} custom-call(bf16[4,64,384]{2,1,0:T(8,128)(2,1)S(1)} %get-tuple-element.190.far, bf16[4,64,384]{2,1,0:T(8,128)(2,1)S(1)} %get-tuple-element.191.near, bf16[2,4,9,384,384]{4,3,2,1,0:T(8,128)(2,1)S(1)} %get-tuple-element.129.blocks), custom_call_target="tpu_custom_call" | custom-call | flops 3019898880 | bytes 11796480 | tf_op jit(solution)/shard_map/own/pallas_call | solution.py:316
  103.2 6.1 %collective-permute-done.17.halo_near = bf16[4,64,384]{2,1,0:T(8,128)(2,1)S(1)} collective-permute-done((bf16[4,64,384]{2,1,0:T(8,128)(2,1)S(1)}, bf16[4,64,384]{2,1,0:T(8,128)(2,1)S(1)}, u32[]{:S(2)}, u32[]{:S(2)}) %collective-permute-start.17) | collective-permute-done | bytes 196640 | tf_op jit(solution)/shard_map/ppermute | solution.py:272
  110.4 5.3 %collective-permute-start.18 = (bf16[4,64,384]{2,1,0:T(8,128)(2,1)S(1)}, bf16[4,64,384]{2,1,0:T(8,128)(2,1)S(1)}, u32[]{:S(2)}, u32[]{:S(2)}) collective-permute-start(bf16[4,64,384]{2,1,0:T(8,128)(2,1)S(1)} %get-tuple-element.195), channel_id=1, source_target_pairs={{0,15},{1,2},{2,1},{3,4},{4,3},{5,6},{6,5},{7,8},{8,7},{9,10},{10,... | collective-permute-start | bytes 589832 | tf_op jit(solution)/shard_map/ppermute | solution.py:272
  117.4 6.6 %collective-permute-done.18.halo = bf16[4,64,384]{2,1,0:T(8,128)(2,1)S(1)} collective-permute-done((bf16[4,64,384]{2,1,0:T(8,128)(2,1)S(1)}, bf16[4,64,384]{2,1,0:T(8,128)(2,1)S(1)}, u32[]{:S(2)}, u32[]{:S(2)}) %collective-permute-start.18) | collective-permute-done | bytes 196640 | tf_op jit(solution)/shard_map/ppermute | solution.py:272
  124.7 3.9 %collective-permute-start.20 = (bf16[4,64,384]{2,1,0:T(8,128)(2,1)S(1)}, bf16[4,64,384]{2,1,0:T(8,128)(2,1)S(1)}, u32[]{:S(2)}, u32[]{:S(2)}) collective-permute-start(bf16[4,64,384]{2,1,0:T(8,128)(2,1)S(1)} %get-tuple-element.208.far), channel_id=1, source_target_pairs={{0,112},{16,32},{32,16},{48,64},{64,48},{80,96},{96,80},{112,0},{1... | collective-permute-start | bytes 589832 | tf_op jit(solution)/shard_map/ppermute | solution.py:272
  131.8 4.4 %collective-permute-done.21.halo_near = bf16[4,64,384]{2,1,0:T(8,128)(2,1)S(1)} collective-permute-done((bf16[4,64,384]{2,1,0:T(8,128)(2,1)S(1)}, bf16[4,64,384]{2,1,0:T(8,128)(2,1)S(1)}, u32[]{:S(2)}, u32[]{:S(2)}) %collective-permute-start.21) | collective-permute-done | bytes 196640 | tf_op jit(solution)/shard_map/ppermute | solution.py:272
  145.3 3.6 %collective-permute-start.24 = (bf16[4,64,384]{2,1,0:T(8,128)(2,1)S(1)}, bf16[4,64,384]{2,1,0:T(8,128)(2,1)S(1)}, u32[]{:S(2)}, u32[]{:S(2)}) collective-permute-start(bf16[4,64,384]{2,1,0:T(8,128)(2,1)S(1)} %get-tuple-element.226.far), channel_id=1, source_target_pairs={{0,112},{16,32},{32,16},{48,64},{64,48},{80,96},{96,80},{112,0},{1... | collective-permute-start | bytes 589832 | tf_op jit(solution)/shard_map/ppermute | solution.py:272
  152.1 6.5 %collective-permute-done.25.halo_near = bf16[4,64,384]{2,1,0:T(8,128)(2,1)S(1)} collective-permute-done((bf16[4,64,384]{2,1,0:T(8,128)(2,1)S(1)}, bf16[4,64,384]{2,1,0:T(8,128)(2,1)S(1)}, u32[]{:S(2)}, u32[]{:S(2)}) %collective-permute-start.25) | collective-permute-done | bytes 196640 | tf_op jit(solution)/shard_map/ppermute | solution.py:272
  159.8 3.4 %collective-permute-start.26 = (bf16[4,64,384]{2,1,0:T(8,128)(2,1)S(1)}, bf16[4,64,384]{2,1,0:T(8,128)(2,1)S(1)}, u32[]{:S(2)}, u32[]{:S(2)}) collective-permute-start(bf16[4,64,384]{2,1,0:T(8,128)(2,1)S(1)} %get-tuple-element.231), channel_id=1, source_target_pairs={{0,15},{1,2},{2,1},{3,4},{4,3},{5,6},{6,5},{7,8},{8,7},{9,10},{10,... | collective-permute-start | bytes 589832 | tf_op jit(solution)/shard_map/ppermute | solution.py:272
  (84 shorter events, 50.1 us)
Async XLA Ops:
  3.0 15.4 %collective-permute-start.1 = (bf16[4,64,384]{2,1,0:T(8,128)(2,1)S(1)}, bf16[4,64,384]{2,1,0:T(8,128)(2,1)S(1)}, u32[]{:S(2)}, u32[]{:S(2)}) collective-permute-start(bf16[4,64,384]{2,1,0:T(8,128)(2,1)S(1)} %get-tuple-element.126.near.refs_1_.refs_2_.refs_3_.refs_6_), channel_id=1, source_target_pairs={{0,16},{16,0},{32,48},{48,32},{64,80},{80,64},{96,112},{112,96},{1... | collective-permute-start | bytes 589832 | tf_op jit(solution)/shard_map/ppermute | solution.py:272
  6.4 13.1 %collective-permute-start = (bf16[4,64,384]{2,1,0:T(8,128)(2,1)S(1)}, bf16[4,64,384]{2,1,0:T(8,128)(2,1)S(1)}, u32[]{:S(2)}, u32[]{:S(2)}) collective-permute-start(bf16[4,64,384]{2,1,0:T(8,128)(2,1)S(1)} %get-tuple-element.125.far.refs_0_.refs_1_.refs_2_.refs_5_), channel_id=1, source_target_pairs={{0,112},{16,32},{32,16},{48,64},{64,48},{80,96},{96,80},{112,0},{1... | collective-permute-start | bytes 589832 | tf_op jit(solution)/shard_map/ppermute | solution.py:272
  19.6 8.5 %collective-permute-start.2 = (bf16[4,64,384]{2,1,0:T(8,128)(2,1)S(1)}, bf16[4,64,384]{2,1,0:T(8,128)(2,1)S(1)}, u32[]{:S(2)}, u32[]{:S(2)}) collective-permute-start(bf16[4,64,384]{2,1,0:T(8,128)(2,1)S(1)} %get-tuple-element.132), channel_id=1, source_target_pairs={{0,15},{1,2},{2,1},{3,4},{4,3},{5,6},{6,5},{7,8},{8,7},{9,10},{10,... | collective-permute-start | bytes 589832 | tf_op jit(solution)/shard_map/ppermute | solution.py:272
  28.8 12.8 %collective-permute-start.4 = (bf16[4,64,384]{2,1,0:T(8,128)(2,1)S(1)}, bf16[4,64,384]{2,1,0:T(8,128)(2,1)S(1)}, u32[]{:S(2)}, u32[]{:S(2)}) collective-permute-start(bf16[4,64,384]{2,1,0:T(8,128)(2,1)S(1)} %get-tuple-element.139.far), channel_id=1, source_target_pairs={{0,112},{16,32},{32,16},{48,64},{64,48},{80,96},{96,80},{112,0},{1... | collective-permute-start | bytes 589832 | tf_op jit(solution)/shard_map/ppermute | solution.py:272
  31.7 8.9 %collective-permute-start.5 = (bf16[4,64,384]{2,1,0:T(8,128)(2,1)S(1)}, bf16[4,64,384]{2,1,0:T(8,128)(2,1)S(1)}, u32[]{:S(2)}, u32[]{:S(2)}) collective-permute-start(bf16[4,64,384]{2,1,0:T(8,128)(2,1)S(1)} %get-tuple-element.140.near), channel_id=1, source_target_pairs={{0,16},{16,0},{32,48},{48,32},{64,80},{80,64},{96,112},{112,96},{1... | collective-permute-start | bytes 589832 | tf_op jit(solution)/shard_map/ppermute | solution.py:272
  41.7 6.7 %collective-permute-start.7 = (bf16[4,64,384]{2,1,0:T(8,128)(2,1)S(1)}, bf16[4,64,384]{2,1,0:T(8,128)(2,1)S(1)}, u32[]{:S(2)}, u32[]{:S(2)}) collective-permute-start(bf16[4,64,384]{2,1,0:T(8,128)(2,1)S(1)} %get-tuple-element.149), channel_id=1, source_target_pairs={{0,1},{1,0},{2,3},{3,2},{4,5},{5,4},{6,7},{7,6},{8,9},{9,8},{10,11... | collective-permute-start | bytes 589832 | tf_op jit(solution)/shard_map/ppermute | solution.py:272
  41.8 11.5 %collective-permute-start.6 = (bf16[4,64,384]{2,1,0:T(8,128)(2,1)S(1)}, bf16[4,64,384]{2,1,0:T(8,128)(2,1)S(1)}, u32[]{:S(2)}, u32[]{:S(2)}) collective-permute-start(bf16[4,64,384]{2,1,0:T(8,128)(2,1)S(1)} %get-tuple-element.144), channel_id=1, source_target_pairs={{0,15},{1,2},{2,1},{3,4},{4,3},{5,6},{6,5},{7,8},{8,7},{9,10},{10,... | collective-permute-start | bytes 589832 | tf_op jit(solution)/shard_map/ppermute | solution.py:272
  54.0 10.7 %collective-permute-start.8 = (bf16[4,64,384]{2,1,0:T(8,128)(2,1)S(1)}, bf16[4,64,384]{2,1,0:T(8,128)(2,1)S(1)}, u32[]{:S(2)}, u32[]{:S(2)}) collective-permute-start(bf16[4,64,384]{2,1,0:T(8,128)(2,1)S(1)} %get-tuple-element.154.far), channel_id=1, source_target_pairs={{0,112},{16,32},{32,16},{48,64},{64,48},{80,96},{96,80},{112,0},{1... | collective-permute-start | bytes 589832 | tf_op jit(solution)/shard_map/ppermute | solution.py:272
  54.3 9.3 %collective-permute-start.9 = (bf16[4,64,384]{2,1,0:T(8,128)(2,1)S(1)}, bf16[4,64,384]{2,1,0:T(8,128)(2,1)S(1)}, u32[]{:S(2)}, u32[]{:S(2)}) collective-permute-start(bf16[4,64,384]{2,1,0:T(8,128)(2,1)S(1)} %get-tuple-element.155.near), channel_id=1, source_target_pairs={{0,16},{16,0},{32,48},{48,32},{64,80},{80,64},{96,112},{112,96},{1... | collective-permute-start | bytes 589832 | tf_op jit(solution)/shard_map/ppermute | solution.py:272
  64.8 10.7 %collective-permute-start.10 = (bf16[4,64,384]{2,1,0:T(8,128)(2,1)S(1)}, bf16[4,64,384]{2,1,0:T(8,128)(2,1)S(1)}, u32[]{:S(2)}, u32[]{:S(2)}) collective-permute-start(bf16[4,64,384]{2,1,0:T(8,128)(2,1)S(1)} %get-tuple-element.159), channel_id=1, source_target_pairs={{0,15},{1,2},{2,1},{3,4},{4,3},{5,6},{6,5},{7,8},{8,7},{9,10},{10,... | collective-permute-start | bytes 589832 | tf_op jit(solution)/shard_map/ppermute | solution.py:272
  76.1 10.6 %collective-permute-start.12 = (bf16[4,64,384]{2,1,0:T(8,128)(2,1)S(1)}, bf16[4,64,384]{2,1,0:T(8,128)(2,1)S(1)}, u32[]{:S(2)}, u32[]{:S(2)}) collective-permute-start(bf16[4,64,384]{2,1,0:T(8,128)(2,1)S(1)} %get-tuple-element.172.far), channel_id=1, source_target_pairs={{0,112},{16,32},{32,16},{48,64},{64,48},{80,96},{96,80},{112,0},{1... | collective-permute-start | bytes 589832 | tf_op jit(solution)/shard_map/ppermute | solution.py:272
  76.5 9.3 %collective-permute-start.13 = (bf16[4,64,384]{2,1,0:T(8,128)(2,1)S(1)}, bf16[4,64,384]{2,1,0:T(8,128)(2,1)S(1)}, u32[]{:S(2)}, u32[]{:S(2)}) collective-permute-start(bf16[4,64,384]{2,1,0:T(8,128)(2,1)S(1)} %get-tuple-element.173.near), channel_id=1, source_target_pairs={{0,16},{16,0},{32,48},{48,32},{64,80},{80,64},{96,112},{112,96},{1... | collective-permute-start | bytes 589832 | tf_op jit(solution)/shard_map/ppermute | solution.py:272
  86.8 6.6 %collective-permute-start.15 = (bf16[4,64,384]{2,1,0:T(8,128)(2,1)S(1)}, bf16[4,64,384]{2,1,0:T(8,128)(2,1)S(1)}, u32[]{:S(2)}, u32[]{:S(2)}) collective-permute-start(bf16[4,64,384]{2,1,0:T(8,128)(2,1)S(1)} %get-tuple-element.183), channel_id=1, source_target_pairs={{0,1},{1,0},{2,3},{3,2},{4,5},{5,4},{6,7},{7,6},{8,9},{9,8},{10,11... | collective-permute-start | bytes 589832 | tf_op jit(solution)/shard_map/ppermute | solution.py:272
  86.9 12.0 %collective-permute-start.14 = (bf16[4,64,384]{2,1,0:T(8,128)(2,1)S(1)}, bf16[4,64,384]{2,1,0:T(8,128)(2,1)S(1)}, u32[]{:S(2)}, u32[]{:S(2)}) collective-permute-start(bf16[4,64,384]{2,1,0:T(8,128)(2,1)S(1)} %get-tuple-element.177), channel_id=1, source_target_pairs={{0,15},{1,2},{2,1},{3,4},{4,3},{5,6},{6,5},{7,8},{8,7},{9,10},{10,... | collective-permute-start | bytes 589832 | tf_op jit(solution)/shard_map/ppermute | solution.py:272
  99.6 10.7 %collective-permute-start.16 = (bf16[4,64,384]{2,1,0:T(8,128)(2,1)S(1)}, bf16[4,64,384]{2,1,0:T(8,128)(2,1)S(1)}, u32[]{:S(2)}, u32[]{:S(2)}) collective-permute-start(bf16[4,64,384]{2,1,0:T(8,128)(2,1)S(1)} %get-tuple-element.190.far), channel_id=1, source_target_pairs={{0,112},{16,32},{32,16},{48,64},{64,48},{80,96},{96,80},{112,0},{1... | collective-permute-start | bytes 589832 | tf_op jit(solution)/shard_map/ppermute | solution.py:272
  99.7 9.6 %collective-permute-start.17 = (bf16[4,64,384]{2,1,0:T(8,128)(2,1)S(1)}, bf16[4,64,384]{2,1,0:T(8,128)(2,1)S(1)}, u32[]{:S(2)}, u32[]{:S(2)}) collective-permute-start(bf16[4,64,384]{2,1,0:T(8,128)(2,1)S(1)} %get-tuple-element.191.near), channel_id=1, source_target_pairs={{0,16},{16,0},{32,48},{48,32},{64,80},{80,64},{96,112},{112,96},{1... | collective-permute-start | bytes 589832 | tf_op jit(solution)/shard_map/ppermute | solution.py:272
  110.3 6.3 %collective-permute-start.19 = (bf16[4,64,384]{2,1,0:T(8,128)(2,1)S(1)}, bf16[4,64,384]{2,1,0:T(8,128)(2,1)S(1)}, u32[]{:S(2)}, u32[]{:S(2)}) collective-permute-start(bf16[4,64,384]{2,1,0:T(8,128)(2,1)S(1)} %get-tuple-element.201), channel_id=1, source_target_pairs={{0,1},{1,0},{2,3},{3,2},{4,5},{5,4},{6,7},{7,6},{8,9},{9,8},{10,11... | collective-permute-start | bytes 589832 | tf_op jit(solution)/shard_map/ppermute | solution.py:272
  110.4 13.5 %collective-permute-start.18 = (bf16[4,64,384]{2,1,0:T(8,128)(2,1)S(1)}, bf16[4,64,384]{2,1,0:T(8,128)(2,1)S(1)}, u32[]{:S(2)}, u32[]{:S(2)}) collective-permute-start(bf16[4,64,384]{2,1,0:T(8,128)(2,1)S(1)} %get-tuple-element.195), channel_id=1, source_target_pairs={{0,15},{1,2},{2,1},{3,4},{4,3},{5,6},{6,5},{7,8},{8,7},{9,10},{10,... | collective-permute-start | bytes 589832 | tf_op jit(solution)/shard_map/ppermute | solution.py:272
  124.7 12.5 %collective-permute-start.20 = (bf16[4,64,384]{2,1,0:T(8,128)(2,1)S(1)}, bf16[4,64,384]{2,1,0:T(8,128)(2,1)S(1)}, u32[]{:S(2)}, u32[]{:S(2)}) collective-permute-start(bf16[4,64,384]{2,1,0:T(8,128)(2,1)S(1)} %get-tuple-element.208.far), channel_id=1, source_target_pairs={{0,112},{16,32},{32,16},{48,64},{64,48},{80,96},{96,80},{112,0},{1... | collective-permute-start | bytes 589832 | tf_op jit(solution)/shard_map/ppermute | solution.py:272
  128.6 7.6 %collective-permute-start.21 = (bf16[4,64,384]{2,1,0:T(8,128)(2,1)S(1)}, bf16[4,64,384]{2,1,0:T(8,128)(2,1)S(1)}, u32[]{:S(2)}, u32[]{:S(2)}) collective-permute-start(bf16[4,64,384]{2,1,0:T(8,128)(2,1)S(1)} %get-tuple-element.209.near), channel_id=1, source_target_pairs={{0,16},{16,0},{32,48},{48,32},{64,80},{80,64},{96,112},{112,96},{1... | collective-permute-start | bytes 589832 | tf_op jit(solution)/shard_map/ppermute | solution.py:272
  137.3 7.3 %collective-permute-start.22 = (bf16[4,64,384]{2,1,0:T(8,128)(2,1)S(1)}, bf16[4,64,384]{2,1,0:T(8,128)(2,1)S(1)}, u32[]{:S(2)}, u32[]{:S(2)}) collective-permute-start(bf16[4,64,384]{2,1,0:T(8,128)(2,1)S(1)} %get-tuple-element.213), channel_id=1, source_target_pairs={{0,15},{1,2},{2,1},{3,4},{4,3},{5,6},{6,5},{7,8},{8,7},{9,10},{10,... | collective-permute-start | bytes 589832 | tf_op jit(solution)/shard_map/ppermute | solution.py:272
  145.3 14.3 %collective-permute-start.24 = (bf16[4,64,384]{2,1,0:T(8,128)(2,1)S(1)}, bf16[4,64,384]{2,1,0:T(8,128)(2,1)S(1)}, u32[]{:S(2)}, u32[]{:S(2)}) collective-permute-start(bf16[4,64,384]{2,1,0:T(8,128)(2,1)S(1)} %get-tuple-element.226.far), channel_id=1, source_target_pairs={{0,112},{16,32},{32,16},{48,64},{64,48},{80,96},{96,80},{112,0},{1... | collective-permute-start | bytes 589832 | tf_op jit(solution)/shard_map/ppermute | solution.py:272
  148.9 9.7 %collective-permute-start.25 = (bf16[4,64,384]{2,1,0:T(8,128)(2,1)S(1)}, bf16[4,64,384]{2,1,0:T(8,128)(2,1)S(1)}, u32[]{:S(2)}, u32[]{:S(2)}) collective-permute-start(bf16[4,64,384]{2,1,0:T(8,128)(2,1)S(1)} %get-tuple-element.227.near), channel_id=1, source_target_pairs={{0,16},{16,0},{32,48},{48,32},{64,80},{80,64},{96,112},{112,96},{1... | collective-permute-start | bytes 589832 | tf_op jit(solution)/shard_map/ppermute | solution.py:272
  159.8 7.3 %collective-permute-start.26 = (bf16[4,64,384]{2,1,0:T(8,128)(2,1)S(1)}, bf16[4,64,384]{2,1,0:T(8,128)(2,1)S(1)}, u32[]{:S(2)}, u32[]{:S(2)}) collective-permute-start(bf16[4,64,384]{2,1,0:T(8,128)(2,1)S(1)} %get-tuple-element.231), channel_id=1, source_target_pairs={{0,15},{1,2},{2,1},{3,4},{4,3},{5,6},{6,5},{7,8},{8,7},{9,10},{10,... | collective-permute-start | bytes 589832 | tf_op jit(solution)/shard_map/ppermute | solution.py:272
  (8 other events, 41.4 us)
